TPU v7x, 32 devices: a whole 2x2x4 slice. The times are simulated.
32 devices in a mesh: gx: 4 (over y, x), gy: 8 (over z, core).
Axes of the slice: x: 2, y: 2, z: 4, core: 2. Of those that a mesh axis runs over, the one named last changes fastest.
Arguments:
- features: bfloat16 [32768, 768], P(('gx', 'gy')), may hold values from -6 to 6
- seed_rows: int32 [2048], P(('gx', 'gy')), may hold values from 0 to 1023
- hop1_ids: int32 [2048, 5], P(('gx', 'gy')), may hold values from 0 to 32767, as said below
- hop2_ids: int32 [2048, 5, 5], P(('gx', 'gy')), may hold values from 0 to 32767, as said below
- w_self: bfloat16 [768, 1024], replicated, may hold values from -0.21875 to 0.21875
- w_neigh: bfloat16 [768, 1024], replicated, may hold values from -0.21875 to 0.21875
- bias: float32 [1024], replicated, may hold values from -3 to 3
- cotangent: bfloat16 [2048, 1024], P(('gx', 'gy')), may hold values from -6 to 6
Outputs:
- embedded: bfloat16 [2048, 1024], P(('gx', 'gy'))
- grad_self: float32 [768, 1024], P(None, ('gx', 'gy'))
- grad_neigh: float32 [768, 1024], P(None, ('gx', 'gy'))
- grad_bias: float32 [1024], P(('gx', 'gy'))
Inputs may be any that keep to these rules, and one draw needn't show every extreme that they name: `hop1_ids`: row i belongs to device i // 1024 (device index gx * 8 + gy). The 320 entries of one device name at most 15 rows of any one owner, repeats counted; in every draw one owner receives exactly 15 from every device. `hop2_ids`: row i belongs to device i // 1024. The 1600 entries of one device name at most 75 rows of any one owner, repeats counted; in every draw one owner receives exactly 75 from every device.
All inputs are finite; a program needn't handle non-finite values.
Results may differ from a plain program's by a relative error of at most 0.025.
The roundings to bfloat16 on the way count: a program that leaves them out, or rounds other values in their place, can miss the bound.
Values may be sent and summed in bfloat16 or wider, within the bound.
A program may use at most 64 MiB of HBM per device.

v0:
```python
import jax
import jax.numpy as jnp
from jax import lax
from jax.sharding import PartitionSpec as P


def contract_rows(left, right):
    return lax.dot_general(
        left, right, (((0,), (0,)), ((), ())), preferred_element_type=jnp.float32
    )


def plan_slots(row_ids, rows_dev, devices, capacity):
    item_count = row_ids.shape[0]
    owners = row_ids // rows_dev
    locals_at = row_ids - owners * rows_dev
    sorted_at = jnp.argsort(owners, stable=True)
    matched = (owners[:, None] == jnp.arange(devices, dtype=jnp.int32)[None, :]).astype(jnp.int32)
    totals = jnp.sum(matched, axis=0)
    starts = jnp.cumsum(totals) - totals
    ranked = jnp.arange(item_count, dtype=jnp.int32) - starts[owners[sorted_at]]
    placed = jnp.zeros((item_count,), jnp.int32).at[sorted_at].set(ranked)
    slot_at = owners * capacity + placed
    request = jnp.full((devices * capacity,), -1, jnp.int32).at[slot_at].set(locals_at)
    return (slot_at, request)


def serve_rows(features, asked):
    return features[jnp.maximum(asked, 0)]


def pool_rows(rows, group):
    width = rows.shape[1]
    summed = jnp.sum(rows.astype(jnp.float32).reshape(-1, group, width), axis=1)
    return (summed / group).astype(jnp.bfloat16)


def layer_pre(rows, pooled, w_self, w_neigh, bias):
    return (
        jnp.dot(rows, w_self, preferred_element_type=jnp.float32)
        + jnp.dot(pooled, w_neigh, preferred_element_type=jnp.float32)
        + bias
    )


def body(features, seed_rows, hop1_ids, hop2_ids, w_self, w_neigh, bias, cotangent):
    split_x = lax.axis_size("gx")
    split_y = lax.axis_size("gy")
    devices = split_x * split_y
    rows_dev = features.shape[0]
    width = features.shape[1]
    hidden_width = w_self.shape[1]
    seeds = seed_rows.shape[0]
    fan_one = hop1_ids.shape[1]
    fan_two = hop2_ids.shape[2]
    near_total = seeds * fan_one
    far_total = near_total * fan_two
    near_cap = max(2, 3 * near_total // (2 * devices))
    far_cap = max(2, 3 * far_total // (2 * devices))
    near_slot, near_request = plan_slots(hop1_ids.reshape(-1), rows_dev, devices, near_cap)
    far_slot, far_request = plan_slots(hop2_ids.reshape(-1), rows_dev, devices, far_cap)
    near_grid = near_request.reshape(split_x, split_y, near_cap)
    far_grid = far_request.reshape(split_x, split_y, far_cap)
    zero_value = jnp.zeros((), jnp.bfloat16)
    asked = (
        lax.all_to_all(
            lax.all_to_all(far_grid, "gx", split_axis=0, concat_axis=0, tiled=True),
            "gy",
            split_axis=1,
            concat_axis=1,
            tiled=True,
        ),
        lax.all_to_all(
            lax.all_to_all(near_grid, "gx", split_axis=0, concat_axis=0, tiled=True),
            "gy",
            split_axis=1,
            concat_axis=1,
            tiled=True,
        ),
    )
    served = (serve_rows(features, asked[0]), serve_rows(features, asked[1]))
    answered = (
        lax.all_to_all(
            lax.all_to_all(served[0], "gx", split_axis=0, concat_axis=0, tiled=True),
            "gy",
            split_axis=1,
            concat_axis=1,
            tiled=True,
        ),
        lax.all_to_all(
            lax.all_to_all(served[1], "gx", split_axis=0, concat_axis=0, tiled=True),
            "gy",
            split_axis=1,
            concat_axis=1,
            tiled=True,
        ),
    )
    far_rows = answered[0].reshape(-1, width)[far_slot]
    near_rows = answered[1].reshape(-1, width)[near_slot]
    pooled_far = pool_rows(far_rows, fan_two)
    near_pre = layer_pre(near_rows, pooled_far, w_self, w_neigh, bias)
    near_hidden = jnp.maximum(near_pre, 0.0).astype(jnp.bfloat16)
    seed_x = features[seed_rows]
    pooled_near = pool_rows(near_rows, fan_one)
    seed_pre = layer_pre(seed_x, pooled_near, w_self, w_neigh, bias)
    seed_hidden = jnp.maximum(seed_pre, 0.0).astype(jnp.bfloat16)
    summed = seed_hidden.astype(jnp.float32) + jnp.sum(
        near_hidden.astype(jnp.float32).reshape(seeds, fan_one, hidden_width), axis=1
    )
    embedded = (summed / (1 + fan_one)).astype(jnp.bfloat16)
    spread = (cotangent.astype(jnp.float32) / (1 + fan_one)).astype(jnp.bfloat16)
    seed_delta = jnp.where(seed_pre > 0, spread, zero_value)
    grad_self = contract_rows(seed_x, seed_delta)
    grad_neigh = contract_rows(pooled_near, seed_delta)
    grad_bias = jnp.sum(seed_delta.astype(jnp.float32), axis=0)
    near_spread = jnp.repeat(spread, fan_one, axis=0)
    near_delta = jnp.where(near_pre > 0, near_spread, zero_value)
    grad_self = grad_self + contract_rows(near_rows, near_delta)
    grad_neigh = grad_neigh + contract_rows(pooled_far, near_delta)
    grad_bias = grad_bias + jnp.sum(near_delta.astype(jnp.float32), axis=0)
    reduced = (
        lax.psum_scatter(grad_self, ("gx", "gy"), scatter_dimension=1, tiled=True),
        lax.psum_scatter(grad_neigh, ("gx", "gy"), scatter_dimension=1, tiled=True),
        lax.psum_scatter(grad_bias, ("gx", "gy"), scatter_dimension=0, tiled=True),
    )
    return (embedded, reduced[0], reduced[1], reduced[2])


def solution(mesh):
    in_specs = (
        P(("gx", "gy"), None),
        P(("gx", "gy")),
        P(("gx", "gy"), None),
        P(("gx", "gy"), None, None),
        P(),
        P(),
        P(),
        P(("gx", "gy"), None),
    )
    out_specs = (
        P(("gx", "gy"), None),
        P(None, ("gx", "gy")),
        P(None, ("gx", "gy")),
        P(("gx", "gy")),
    )
    return jax.shard_map(body, mesh=mesh, in_specs=in_specs, out_specs=out_specs, check_vma=False)
```

profile of v0, /device:TPU:11, one launch (start us, length us, event | category | flops | bytes accessed | tf_op | source)
XLA Modules:
  0.0 566.6 jit_solution(34076304562649905)
XLA Ops:
  10.1 3.8 sort.34
  16.3 4.3 fusion.13
  20.8 15.8 %select_subtract_fusion.1 = s32[320]{0:T(512)S(1)} fusion(pred[320]{0:T(512)(128)(4,1)S(1)} %get-tuple-element.57, pred[320]{0:T(512)(128)(4,1)S(1)} %get-tuple-element.56, pred[320]{0:T(512)(128)(4,1)S(1)} %get-tuple-element.55, pred[320]{0:T(512)(128)(4,1)S(1)} %get-tuple-element.54, pred[320]{0:T(512)(128)(4,1)S(1)} %get-tuple-element.53, ...), kind=kLoop, calls=%fused_computation.130 | loop fusion | flops 8320 | bytes 10660 | tf_op jit(solution)/shard_map/sub | solution.py:21
  43.1 3.7 all-to-all-start
  49.1 5.0 sort.35
  54.1 8.8 %gather_fusion.4 = s32[1600]{0:T(1024)S(1)} fusion(s32[1600]{0:T(1024)S(1)} %add_select_fusion, s32[2048]{0:T(1024)S(1)} %pad_clamp_fusion.2), kind=kCustom, calls=%fused_computation.4 | custom fusion | bytes 19200 | tf_op jit(solution)/shard_map/gather | solution.py:21
  62.9 4.3 fusion.6
  67.8 15.8 %select_subtract_fusion = s32[1600]{0:T(1024)S(1)} fusion(pred[1600]{0:T(1024)(128)(4,1)S(1)} %get-tuple-element.32, pred[1600]{0:T(1024)(128)(4,1)S(1)} %get-tuple-element.31, pred[1600]{0:T(1024)(128)(4,1)S(1)} %get-tuple-element.30, pred[1600]{0:T(1024)(128)(4,1)S(1)} %get-tuple-element.29, pred[1600]{0:T(1024)(128)(4,1)S(1)} %get-tuple-element.28, ...), kind=kLoop, calls=%fused_computation.78 | loop fusion | flops 41600 | bytes 52900 | tf_op jit(solution)/shard_map/sub | solution.py:21
  83.6 8.8 %scatter_custom_fusion.2 = s32[1600]{0:T(1024)S(1)} fusion(s32[1600]{0:T(1024)S(1)} %compare_select_fusion.10, s32[1600]{0:T(1024)S(1)} %select_subtract_fusion, s32[]{:T(128)} %constant.24.clone.1), kind=kCustom, calls=%fused_computation.122 | custom fusion | bytes 6404 | tf_op jit(solution)/shard_map/scatter | solution.py:22
  93.0 6.2 %all-to-all-start.1 = ((s32[4,8,15]{2,0,1:T(4,128)}), s32[4,8,15]{2,0,1:T(4,128)S(1)}, u32[]{:S(2)}, u32[]{:S(2)}) async-start(s32[4,8,15]{2,0,1:T(4,128)} %copy.58), calls=%async_computation.1 | async-start | bytes 32768 | tf_op jit(solution)/shard_map/all_to_all | solution.py:73
  99.2 8.8 %scatter_custom_fusion.3 = s32[2400]{0:T(1024)S(1)} fusion(s32[1600]{0:T(1024)S(1)} %get-tuple-element.71, s32[1600]{0:T(1024)S(1)} %get-tuple-element.70, s32[]{:T(128)} %constant.26.clone.1), kind=kCustom, calls=%fused_computation.83 | custom fusion | bytes 9604 | tf_op jit(solution)/shard_map/scatter | solution.py:24
  108.7 3.6 all-to-all-start.4
  115.4 6.5 %all-to-all-start.5 = ((s32[4,8,75]{2,0,1:T(4,128)}), s32[4,8,75]{2,0,1:T(4,128)S(1)}, u32[]{:S(2)}, u32[]{:S(2)}) async-start(s32[4,8,75]{2,0,1:T(4,128)} %copy.65), calls=%async_computation.5 | async-start | bytes 32768 | tf_op jit(solution)/shard_map/all_to_all | solution.py:66
  125.8 4.6 all-to-all-start.2
  130.5 8.5 %gather_fusion.5 = bf16[2400,768]{1,0:T(8,128)(2,1)} fusion(bf16[1024,768]{1,0:T(8,128)(2,1)S(1)} %copy-done, s32[3072]{0:T(1024)S(1)} %pad_clamp_fusion), kind=kCustom, calls=%fused_computation.5 | custom fusion | bytes 7382400 | tf_op jit(solution)/shard_map/gather | solution.py:29
  139.0 4.9 reshape.314
  144.0 5.3 copy.67
  149.2 5.0 all-to-all-start.6
  155.3 39.9 %all-to-all-done.6 = bf16[4,8,75,768]{3,1,2,0:T(8,128)(2,1)} async-done(((bf16[4,8,75,768]{3,1,2,0:T(8,128)(2,1)}), bf16[4,8,75,768]{3,1,2,0:T(8,128)(2,1)}, u32[]{:S(2)}, u32[]{:S(2)}) %all-to-all-start.6) | async-done | bytes 3686432 | tf_op jit(solution)/shard_map/all_to_all | solution.py:84
  195.3 6.0 %all-to-all-start.3 = ((bf16[4,8,15,768]{3,0,2,1:T(4,128)(2,1)}), bf16[4,8,15,768]{3,0,2,1:T(4,128)(2,1)S(1)}, u32[]{:S(2)}, u32[]{:S(2)}) async-start(bf16[4,8,15,768]{3,0,2,1:T(4,128)(2,1)} %copy.61), calls=%async_computation.3 | async-start | bytes 1474560 | tf_op jit(solution)/shard_map/all_to_all | solution.py:90
  201.3 5.3 copy.68
  206.6 11.1 %all-to-all-done.3 = bf16[4,8,15,768]{3,0,2,1:T(4,128)(2,1)S(1)} async-done(((bf16[4,8,15,768]{3,0,2,1:T(4,128)(2,1)}), bf16[4,8,15,768]{3,0,2,1:T(4,128)(2,1)S(1)}, u32[]{:S(2)}, u32[]{:S(2)}) %all-to-all-start.3) | async-done | bytes 737312 | tf_op jit(solution)/shard_map/all_to_all | solution.py:90
  217.7 7.9 %all-to-all-start.7 = ((bf16[4,8,75,768]{3,0,2,1:T(4,128)(2,1)}), bf16[4,8,75,768]{3,0,2,1:T(4,128)(2,1)}, u32[]{:S(2)}, u32[]{:S(2)}) async-start(bf16[4,8,75,768]{3,0,2,1:T(4,128)(2,1)} %copy.68), calls=%async_computation.7 | async-start | bytes 7372800 | tf_op jit(solution)/shard_map/all_to_all | solution.py:83
  235.3 69.9 %all-to-all-done.7 = bf16[4,8,75,768]{3,0,2,1:T(4,128)(2,1)} async-done(((bf16[4,8,75,768]{3,0,2,1:T(4,128)(2,1)}), bf16[4,8,75,768]{3,0,2,1:T(4,128)(2,1)}, u32[]{:S(2)}, u32[]{:S(2)}) %all-to-all-start.7) | async-done | bytes 3686432 | tf_op jit(solution)/shard_map/all_to_all | solution.py:83
  305.2 4.4 copy.69
  309.6 5.0 reshape.187
  314.6 10.0 %gather_fusion.6 = bf16[1600,768]{1,0:T(8,128)(2,1)} fusion(bf16[2400,768]{1,0:T(8,128)(2,1)} %reshape.187, s32[2048]{0:T(1024)S(1)} %pad_clamp_fusion.1), kind=kCustom, calls=%fused_computation.6 | custom fusion | bytes 4921600 | tf_op jit(solution)/shard_map/gather | solution.py:98
  324.6 5.9 %reshape.192 = f32[320,5,768]{2,1,0:T(8,128)} reshape(bf16[1600,768]{1,0:T(8,128)(2,1)} %gather_fusion.6) | data formatting | bytes 7372800 | tf_op jit(solution)/shard_map/convert_element_type | solution.py:34
  330.5 5.7 %reduce_sum.66 = f32[320,768]{1,0:T(8,128)S(1)} reduce(f32[320,5,768]{2,1,0:T(8,128)} %reshape.192, f32[]{:T(128)} %constant.68.clone.1), dimensions={1}, to_apply=%region_11.12 | reduce | flops 983040 | bytes 5898244 | tf_op jit(solution)/shard_map/reduce_sum | solution.py:34
  355.8 41.1 %all-reduce = f32[1024]{0:T(1024)S(1)} all-reduce(f32[1024]{0:T(1024)S(1)} %add.129), channel_id=4, replica_groups=mesh['gx'=4,'gy'=8] {'gx','gy'}, use_global_device_ids=true, to_apply=%region_17.18.clone | all-reduce | flops 1024 | bytes 8192
  397.5 55.1 %reduce-scatter.5.cloned.1.call-done = f32[768,32]{0,1:T(8,128)} async-done(((f32[768,1024]{0,1:T(8,128)}), f32[768,32]{0,1:T(8,128)}) %reduce-scatter.5.cloned.1.call-update) | async-done | bytes 98320 | tf_op jit(solution)/shard_map/reduce_scatter | solution.py:123
  452.6 107.2 %reduce-scatter.3.cloned.1.call-done = f32[768,32]{0,1:T(8,128)} async-done(((f32[768,1024]{0,1:T(8,128)}), f32[768,32]{0,1:T(8,128)}) %reduce-scatter.3.cloned.1.call-update) | async-done | bytes 98320 | tf_op jit(solution)/shard_map/reduce_scatter | solution.py:122
  (105 shorter events, 54.0 us)
Async XLA Ops:
  7.2 114.7 %copy-start = (bf16[1024,768]{1,0:T(8,128)(2,1)S(1)}, bf16[1024,768]{1,0:T(8,128)(2,1)}, u32[]{:S(2)}) copy-start(bf16[1024,768]{1,0:T(8,128)(2,1)} %param.8) | copy-start | bytes 4718596
  7.2 39.6 %copy-start.9 = (s32[64,5,5]{0,2,1:T(8,128)S(1)}, s32[64,5,5]{0,2,1:T(8,128)}, u32[]{:S(2)}) copy-start(s32[64,5,5]{0,2,1:T(8,128)} %param.11) | copy-start | bytes 19204
  43.1 49.3 %all-to-all-start = ((s32[4,8,15]{2,1,0:T(8,128)}), s32[4,8,15]{2,1,0:T(8,128)S(1)}, u32[]{:S(2)}, u32[]{:S(2)}) async-start(s32[4,8,15]{2,1,0:T(8,128)} %reshape.181), calls=%async_computation | async-start | bytes 32768 | tf_op jit(solution)/shard_map/all_to_all | solution.py:74
  93.0 15.7 %all-to-all-start.1 = ((s32[4,8,15]{2,0,1:T(4,128)}), s32[4,8,15]{2,0,1:T(4,128)S(1)}, u32[]{:S(2)}, u32[]{:S(2)}) async-start(s32[4,8,15]{2,0,1:T(4,128)} %copy.58), calls=%async_computation.1 | async-start | bytes 32768 | tf_op jit(solution)/shard_map/all_to_all | solution.py:73
  108.7 6.1 %all-to-all-start.4 = ((s32[4,8,75]{2,1,0:T(8,128)}), s32[4,8,75]{2,1,0:T(8,128)S(1)}, u32[]{:S(2)}, u32[]{:S(2)}) async-start(s32[4,8,75]{2,1,0:T(8,128)} %reshape.186), calls=%async_computation.4 | async-start | bytes 32768 | tf_op jit(solution)/shard_map/all_to_all | solution.py:67
  115.4 10.5 %all-to-all-start.5 = ((s32[4,8,75]{2,0,1:T(4,128)}), s32[4,8,75]{2,0,1:T(4,128)S(1)}, u32[]{:S(2)}, u32[]{:S(2)}) async-start(s32[4,8,75]{2,0,1:T(4,128)} %copy.65), calls=%async_computation.5 | async-start | bytes 32768 | tf_op jit(solution)/shard_map/all_to_all | solution.py:66
  125.8 23.4 %all-to-all-start.2 = ((bf16[4,8,15,768]{3,1,2,0:T(8,128)(2,1)}), bf16[4,8,15,768]{3,1,2,0:T(8,128)(2,1)S(1)}, u32[]{:S(2)}, u32[]{:S(2)}) async-start(bf16[4,8,15,768]{3,1,2,0:T(8,128)(2,1)} %copy.60), calls=%async_computation.2 | async-start | bytes 1474560 | tf_op jit(solution)/shard_map/all_to_all | solution.py:91
  149.2 46.0 %all-to-all-start.6 = ((bf16[4,8,75,768]{3,1,2,0:T(8,128)(2,1)}), bf16[4,8,75,768]{3,1,2,0:T(8,128)(2,1)}, u32[]{:S(2)}, u32[]{:S(2)}) async-start(bf16[4,8,75,768]{3,1,2,0:T(8,128)(2,1)} %copy.67), calls=%async_computation.6 | async-start | bytes 7372800 | tf_op jit(solution)/shard_map/all_to_all | solution.py:84
  195.3 22.4 %all-to-all-start.3 = ((bf16[4,8,15,768]{3,0,2,1:T(4,128)(2,1)}), bf16[4,8,15,768]{3,0,2,1:T(4,128)(2,1)S(1)}, u32[]{:S(2)}, u32[]{:S(2)}) async-start(bf16[4,8,15,768]{3,0,2,1:T(4,128)(2,1)} %copy.61), calls=%async_computation.3 | async-start | bytes 1474560 | tf_op jit(solution)/shard_map/all_to_all | solution.py:90
  206.6 19.0 %copy-start.11 = (s32[64]{0:T(128)S(1)}, s32[64]{0:T(128)}, u32[]{:S(2)}) copy-start(s32[64]{0:T(128)} %param.9) | copy-start | bytes 772
  217.7 87.5 %all-to-all-start.7 = ((bf16[4,8,75,768]{3,0,2,1:T(4,128)(2,1)}), bf16[4,8,75,768]{3,0,2,1:T(4,128)(2,1)}, u32[]{:S(2)}, u32[]{:S(2)}) async-start(bf16[4,8,75,768]{3,0,2,1:T(4,128)(2,1)} %copy.68), calls=%async_computation.7 | async-start | bytes 7372800 | tf_op jit(solution)/shard_map/all_to_all | solution.py:83
  225.6 227.0 %reduce-scatter.5.cloned.1.call-start = ((), (), s32[]{:S(2)}) async-start(), calls=%async_computation.11 | async-start | bytes 3244032 | tf_op jit(solution)/shard_map/reduce_scatter | solution.py:123
  226.3 2.7 copy-start.6
  231.4 0.8 copy-start.4
  330.5 5.7 %copy-start.2 = (bf16[768,1024]{1,0:T(8,128)(2,1)S(1)}, bf16[768,1024]{1,0:T(8,128)(2,1)}, u32[]{:S(2)}) copy-start(bf16[768,1024]{1,0:T(8,128)(2,1)} %param.13) | copy-start | bytes 4718596
  330.5 5.7 %copy-start.10 = (f32[1024]{0:T(1024)S(1)}, f32[1024]{0:T(1024)}, u32[]{:S(2)}) copy-start(f32[1024]{0:T(1024)} %param.14) | copy-start | bytes 12292
  342.4 2.3 copy-start.8
  347.2 1.3 copy-start.3
  351.5 0.9 copy-start.7
  351.6 1.5 copy-start.5
  351.6 208.2 %reduce-scatter.3.cloned.1.call-start = ((), (), s32[]{:S(2)}) async-start(), calls=%async_computation.10 | async-start | bytes 3244032 | tf_op jit(solution)/shard_map/reduce_scatter | solution.py:122
  355.8 204.0 %copy-start.1 = (bf16[1024,768]{1,0:T(8,128)(2,1)S(1)}, bf16[1024,768]{1,0:T(8,128)(2,1)}, u32[]{:S(2)}) copy-start(bf16[1024,768]{1,0:T(8,128)(2,1)} %param.8) | copy-start | bytes 4718596
Sparse Core Ops, SparseCore 0:
  351.7 100.8 reduce-scatter.4
  458.6 101.1 reduce-scatter.2
where the time goes:
time: 572 us; the launch traced here: 567 us
  waiting for transfers between devices  286 us (50%)
  local copies, waits for them, and re-layouts  105 us (18%)
  other arithmetic  59 us (10%)
  starting transfers between devices  43.6 us (8%)
  blocking collectives  41.1 us (7%)
  matrix products  18 us (3%)
  between operations  14.5 us (3%)
    reduce_scatter x1, waiting for transfers between devices, body(): lax.psum_scatter(grad_self, ('gx', 'gy'), scatter_dimension=1, tiled=True)  107 us
    all_to_all x1, waiting for transfers between devices, body(): lax.all_to_all(lax.all_to_all(served[0], 'gx', split_axis=0, concat_axis=...  69.9 us
    reduce_scatter x1, waiting for transfers between devices, body(): lax.psum_scatter(grad_neigh, ('gx', 'gy'), scatter_dimension=1, tiled=True)  55.1 us
    unnamed x1, blocking collectives  41.1 us
    all_to_all x1, waiting for transfers between devices, body(): lax.all_to_all(served[0], 'gx', split_axis=0, concat_axis=0, tiled=True)  39.9 us
    sub x2, other arithmetic, plan_slots(): ranked = jnp.arange(item_count, dtype=jnp.int32) - starts[owners[sorted_at]]  31.6 us
    gather x6, local copies, waits for them, and re-layouts, serve_rows(): return features[jnp.maximum(asked, 0)]  22.1 us
    gather x6, local copies, waits for them, and re-layouts, plan_slots(): ranked = jnp.arange(item_count, dtype=jnp.int32) - starts[owners[sorted_at]]  14.1 us
  transfers between devices with their start and end apart: 10, of which 7 were waited for; matrix products, arithmetic and copies ran while one was open for 17% of the time, Pallas kernels for 0%

commit v1 on v0

v1 whole, which is shorter than its diff:
```python
import functools

import jax
import jax.numpy as jnp
from jax import lax
from jax.experimental import pallas as pl
from jax.experimental.pallas import tpu as pltpu
from jax.sharding import PartitionSpec as P

MESH = pl.DeviceIdType.MESH


def exchange_kernel(split_x, split_y, x_ref, o_ref, own_sem, send_sem, recv_sem):
    devices = split_x * split_y
    me = lax.axis_index("gx") * split_y + lax.axis_index("gy")

    def copy_to(peer):
        return pltpu.make_async_remote_copy(
            src_ref=x_ref.at[peer],
            dst_ref=o_ref.at[me],
            send_sem=send_sem.at[peer],
            recv_sem=recv_sem.at[me],
            device_id=(peer // split_y, lax.rem(peer, split_y)),
            device_id_type=MESH,
        )

    def copy_from(peer):
        return pltpu.make_async_remote_copy(
            src_ref=x_ref.at[peer],
            dst_ref=o_ref.at[peer],
            send_sem=send_sem.at[peer],
            recv_sem=recv_sem.at[peer],
            device_id=(peer // split_y, lax.rem(peer, split_y)),
            device_id_type=MESH,
        )

    own = pltpu.make_async_copy(x_ref.at[me], o_ref.at[me], own_sem)
    own.start()
    barrier = pltpu.get_barrier_semaphore()

    @pl.loop(1, devices)
    def _(k):
        peer = lax.rem(me + k, devices)
        pl.semaphore_signal(
            barrier,
            inc=1,
            device_id=(peer // split_y, lax.rem(peer, split_y)),
            device_id_type=MESH,
        )

    pl.semaphore_wait(barrier, devices - 1)

    @pl.loop(1, devices)
    def _(k):
        copy_to(lax.rem(me + k, devices)).start()

    @pl.loop(1, devices)
    def _(k):
        copy_from(lax.rem(me + devices - k, devices)).wait_recv()

    @pl.loop(1, devices)
    def _(k):
        copy_to(lax.rem(me + k, devices)).wait_send()

    own.wait()


def exchange(x, split_x, split_y, name, number):
    devices = split_x * split_y
    return pl.pallas_call(
        functools.partial(exchange_kernel, split_x, split_y),
        out_shape=jax.ShapeDtypeStruct(x.shape, x.dtype),
        in_specs=[pl.BlockSpec(memory_space=pl.ANY)],
        out_specs=pl.BlockSpec(memory_space=pl.ANY),
        scratch_shapes=[
            pltpu.SemaphoreType.DMA,
            pltpu.SemaphoreType.DMA((devices,)),
            pltpu.SemaphoreType.DMA((devices,)),
        ],
        compiler_params=pltpu.CompilerParams(collective_id=number, has_side_effects=True),
        name=name,
    )(x)


def one_hot(ids, size):
    return (ids[:, None] == jnp.arange(size, dtype=jnp.int32)[None, :]).astype(jnp.bfloat16)


def matmul(left, right):
    return jnp.dot(left, right, preferred_element_type=jnp.float32)


def body(features, seed_rows, hop1_ids, hop2_ids, w_self, w_neigh, bias, cotangent):
    split_x = lax.axis_size("gx")
    split_y = lax.axis_size("gy")
    devices = split_x * split_y
    rows_dev, width = features.shape
    hidden_width = w_self.shape[1]
    seeds = seed_rows.shape[0]
    fan_one = hop1_ids.shape[1]
    fan_two = hop2_ids.shape[2]
    near_total = seeds * fan_one
    far_total = near_total * fan_two
    near_cap = max(2, 3 * near_total // (2 * devices))
    far_cap = max(2, 3 * far_total // (2 * devices))
    cap = -(-(near_cap + far_cap) // 16) * 16
    lanes = -(-cap // 128) * 128
    bf16 = jnp.bfloat16

    ids = jnp.concatenate([hop2_ids.reshape(-1), hop1_ids.reshape(-1)])
    items = far_total + near_total
    owners = ids // rows_dev
    local = ids - owners * rows_dev
    at = jnp.arange(items, dtype=jnp.int32)
    is_near = at >= far_total
    owned = (jnp.arange(devices, dtype=jnp.int32)[:, None] == owners[None, :]).astype(bf16)
    earlier = ((at[:, None] < at[None, :]) & (is_near[:, None] == is_near[None, :])).astype(bf16)
    ranks = jnp.sum(matmul(owned, earlier) * owned.astype(jnp.float32), axis=0).astype(jnp.int32)
    place = jnp.where(is_near, far_cap, 0) + ranks
    high = (local // 128).astype(bf16)
    low = (local % 128).astype(bf16)
    split_ids = matmul(
        jnp.concatenate([owned * high[None, :], owned * low[None, :]], axis=0), one_hot(place, lanes)
    )
    request = (split_ids[:devices] * 128.0 + split_ids[devices:]).astype(jnp.int32)
    request = jnp.broadcast_to(request[:, None, :], (devices, 8, lanes))
    asked = exchange(request, split_x, split_y, "ask", 0)[:, 0, :cap].reshape(-1)

    served = matmul(one_hot(asked, rows_dev), features).astype(bf16)
    rows = exchange(served.reshape(devices, cap, width), split_x, split_y, "answer", 1)
    rows = rows.reshape(devices * cap, width)

    slots = owners * cap + place
    far_slots = slots[:far_total].reshape(near_total, fan_two)
    near_slots = slots[far_total:]
    column = jnp.arange(devices * cap, dtype=jnp.int32)[None, :]
    far_pick = sum((far_slots[:, j : j + 1] == column).astype(jnp.float32) for j in range(fan_two)).astype(bf16)
    pooled_far = (matmul(far_pick, rows) / fan_two).astype(bf16)
    near_rows = matmul(one_hot(near_slots, devices * cap), rows).astype(bf16)
    seed_x = matmul(one_hot(seed_rows, rows_dev), features).astype(bf16)
    summed_near = jnp.sum(near_rows.astype(jnp.float32).reshape(seeds, fan_one, width), axis=1)
    pooled_near = (summed_near / fan_one).astype(bf16)

    x = jnp.concatenate(
        [
            jnp.concatenate([seed_x, near_rows], axis=0),
            jnp.concatenate([pooled_near, pooled_far], axis=0),
        ],
        axis=1,
    )
    pre = matmul(x, jnp.concatenate([w_self, w_neigh], axis=0)) + bias
    hidden = jnp.maximum(pre, 0.0).astype(bf16).astype(jnp.float32)
    summed = hidden[:seeds] + jnp.sum(hidden[seeds:].reshape(seeds, fan_one, hidden_width), axis=1)
    embedded = (summed / (1 + fan_one)).astype(bf16)
    spread = (cotangent.astype(jnp.float32) / (1 + fan_one)).astype(bf16)
    spread = jnp.concatenate([spread, jnp.repeat(spread, fan_one, axis=0)], axis=0)
    delta = jnp.where(pre > 0, spread, jnp.zeros((), bf16))

    ones = jnp.ones((x.shape[0], 128), bf16)
    shares = lax.dot_general(
        delta,
        jnp.concatenate([x, ones], axis=1),
        (((0,), (0,)), ((), ())),
        preferred_element_type=jnp.float32,
    ).astype(bf16)
    block = hidden_width // devices
    shares = exchange(shares.reshape(devices, block, -1), split_x, split_y, "share", 2)
    total = jnp.sum(shares.astype(jnp.float32), axis=0)
    return (
        embedded,
        total[:, :width].T,
        total[:, width : 2 * width].T,
        total[:, 2 * width],
    )


def solution(mesh):
    in_specs = (
        P(("gx", "gy"), None),
        P(("gx", "gy")),
        P(("gx", "gy"), None),
        P(("gx", "gy"), None, None),
        P(),
        P(),
        P(),
        P(("gx", "gy"), None),
    )
    out_specs = (
        P(("gx", "gy"), None),
        P(None, ("gx", "gy")),
        P(None, ("gx", "gy")),
        P(("gx", "gy")),
    )
    return jax.shard_map(body, mesh=mesh, in_specs=in_specs, out_specs=out_specs, check_vma=False)
```

time: 572 us -> 251 us (0.44)
  waiting for transfers between devices: 286 us -> 0 us
  Pallas kernels: 0 us -> 202 us
  local copies, waits for them, and re-layouts: 105 us -> 9.67 us
  other arithmetic: 59 us -> 7.4 us
  starting transfers between devices: 43.6 us -> 0 us
  blocking collectives: 41.1 us -> 0 us
  between operations: 14.5 us -> 0.91 us
  matrix products: 18 us -> 30.9 us
    pallas_call x0 -> x3, Pallas kernels: none -> 202 us  [exchange(): pl.pallas_call(functools.partial(exchange_kernel, split_x, split_y), out_...]
    reduce_scatter x2 -> x0, waiting for transfers between devices: 162 us -> none  [the longest x1 107 us: body(): lax.psum_scatter(grad_self, ('gx', 'gy'), scatter_dimension=1, tiled=True)]
    all_to_all x8 -> x0, waiting for transfers between devices: 124 us -> none  [the longest x1 69.9 us: body(): lax.all_to_all(lax.all_to_all(served[0], 'gx', split_axis=0, concat_axis=...]
    gather x15 -> x0, local copies, waits for them, and re-layouts: 49.1 us -> none  [the longest x6 22.1 us: serve_rows(): return features[jnp.maximum(asked, 0)]]
    all_to_all x8 -> x0, starting transfers between devices: 43.5 us -> none  [the longest x1 7.92 us: body(): lax.all_to_all(lax.all_to_all(served[0], 'gx', split_axis=0, concat_axis=...]
    unnamed x1 -> x0, blocking collectives: 41.1 us -> none
    sub x6 -> x0, other arithmetic: 31.6 us -> none  [the longest x2 31.6 us: plan_slots(): ranked = jnp.arange(item_count, dtype=jnp.int32) - starts[owners[sorted_at]]]
    scatter x4 -> x0, local copies, waits for them, and re-layouts: 23.4 us -> none  [the longest x2 11.7 us: plan_slots(): jnp.full((devices * capacity,), -1, jnp.int32).at[slot_at].set(locals_at)]
  transfers between devices with their start and end apart: 10 -> 0, of which waited for: 7 -> 0; matrix products, arithmetic and copies ran while one was open for 17% -> 0% of each run, Pallas kernels for 0% -> 0%
where the time goes in v1:
time: 251 us
  Pallas kernels  202 us (80%)
  matrix products  30.9 us (12%)
  local copies, waits for them, and re-layouts  9.67 us (4%)
  other arithmetic  7.4 us (3%)
    pallas_call x3, Pallas kernels, exchange(): pl.pallas_call(functools.partial(exchange_kernel, split_x, split_y), out_...  202 us
    dot_general x7, matrix products, matmul(): return jnp.dot(left, right, preferred_element_type=jnp.float32)  25.4 us
    dot_general x1, matrix products, body(): lax.dot_general(delta, jnp.concatenate([x, ones], axis=1), (((0,), (0,)),...  5.49 us

profile of v1, /device:TPU:11, one launch (start us, length us, event | category | flops | bytes accessed | tf_op | source)
XLA Modules:
  0.0 250.9 jit_solution(4415572592031732401)
XLA Ops:
  0.6 1.0 copy.12
  1.7 0.2 reshape.250
  1.9 0.8 copy.13
  2.6 0.1 reshape.251
  3.0 1.8 fusion.41
  4.8 0.5 fusion.44
  5.3 0.7 broadcast_in_dim.18.x_ref
  5.9 10.3 %ask.1 = s32[32,8,128]{2,1,0:T(8,128)} custom-call(s32[32,8,128]{2,1,0:T(8,128)} %broadcast_in_dim.18.x_ref), custom_call_target="tpu_custom_call" | custom-call | tf_op jit(solution)/shard_map/ask/pallas_call | solution.py:70
  16.2 0.9 slice_reduce_fusion.6
  17.3 7.5 %fusion.7 = bf16[3072,768]{1,0:T(8,128)(2,1)} fusion(bf16[1024,768]{1,0:T(8,128)(2,1)S(1)} %copy-done, s32[3072]{0:T(1024)S(1)} %eq.172), kind=kOutput, calls=%fused_computation.9 | convolution fusion | flops 4837343232 | bytes 6303744 | tf_op jit(solution)/shard_map/dot_general | solution.py:90
  24.8 111.2 %answer.1 = bf16[32,96,768]{2,1,0:T(8,128)(2,1)} custom-call(bf16[32,96,768]{2,1,0:T(8,128)(2,1)} %bitcast.15), custom_call_target="tpu_custom_call" | custom-call | tf_op jit(solution)/shard_map/answer/pallas_call | solution.py:70
  136.0 0.2 convert_element_type.104
  136.2 0.2 concatenate.66
  136.5 0.2 fusion.64
  136.6 0.5 slice_reduce_fusion.4
  137.2 7.2 %fusion.25 = bf16[320,768]{1,0:T(8,128)(2,1)} fusion(bf16[3072,768]{1,0:T(8,128)(2,1)} %bitcast.11, s32[320]{0:T(512)S(1)} %get-tuple-element.5, s32[320]{0:T(512)S(1)} %get-tuple-element.6, s32[320]{0:T(512)S(1)} %get-tuple-element.7, s32[320]{0:T(512)S(1)} %get-tuple-element.8, s32[320]{0:T(512)S(1)} %get-tuple-element.4), kind=kOutput, calls=%fused_computation.35 | convolution fusion | flops 1525186560 | bytes 5216512 | tf_op jit(solution)/shard_map/dot_general | solution.py:90
  144.5 2.7 %fusion.24 = bf16[320,768]{1,0:T(8,128)(2,1)} fusion(bf16[3072,768]{1,0:T(8,128)(2,1)S(1)} %bitcast.14, s32[320]{0:T(512)S(1)} %slice_add_fusion.2), kind=kOutput, calls=%fused_computation.34 | convolution fusion | flops 1511178240 | bytes 5211392 | tf_op jit(solution)/shard_map/dot_general | solution.py:90
  147.2 1.5 reshape.260
  148.7 0.5 reduce_sum.37
  149.2 0.4 convolution_convert_fusion.1
  149.6 5.3 %fusion.45 = (f32[384,1024]{1,0:T(8,128)}, f32[384,1024]{1,0:T(8,128)}) fusion(f32[1024]{0:T(1024)S(1)} %copy-done.5, bf16[768,1024]{1,0:T(8,128)(2,1)} %param.13, bf16[768,1024]{1,0:T(8,128)(2,1)} %param.12, bf16[320,768]{1,0:T(8,128)(2,1)} %fusion.25, bf16[64,768]{1,0:T(8,128)(2,1)S(1)} %multiply_convert_fusion.1, bf16[320,768]{1,0:T(8,128)(2,1)} %fusion.24, ...), kind=kOutput, calls=%fused_computation.55 | convolution fusion | flops 1220542464 | bytes 7475200 | tf_op jit(solution)/shard_map/dot_general | solution.py:90
  154.9 0.2 broadcast_in_dim.20
  155.1 0.3 reshape.257
  155.4 5.5 %convolution_convert_fusion = bf16[1024,1664]{1,0:T(8,128)(2,1)} fusion(bf16[320,768]{1,0:T(8,128)(2,1)} %fusion.25, bf16[64,768]{1,0:T(8,128)(2,1)} %copy-done.3, bf16[320,768]{1,0:T(8,128)(2,1)} %fusion.24, bf16[64,768]{1,0:T(8,128)(2,1)S(1)} %convolution_convert_fusion.1, f32[384,1024]{1,0:T(8,128)} %get-tuple-element.18, ...), kind=kOutput, calls=%fused_computation.18 | convolution fusion | flops 1319469056 | bytes 6954240 | tf_op jit(solution)/shard_map/dot_general | solution.py:160
  160.9 80.5 %share.1 = bf16[32,32,1664]{2,1,0:T(8,128)(2,1)} custom-call(bf16[32,32,1664]{2,1,0:T(8,128)(2,1)} %bitcast.16), custom_call_target="tpu_custom_call" | custom-call | tf_op jit(solution)/shard_map/share/pallas_call | solution.py:70
  241.4 2.6 %convert_reduce_fusion = f32[32,1664]{1,0:T(8,128)S(1)} fusion(bf16[32,32,1664]{2,1,0:T(8,128)(2,1)} %share.1), kind=kLoop, calls=%fused_computation.7 | loop fusion | flops 3354624 | bytes 3620864 | tf_op jit(solution)/shard_map/reduce_sum | solution.py:168
  244.0 0.7 slice_bitcast_fusion
  244.7 0.6 slice_reduce_fusion.5
  245.3 0.1 slice.73
  245.5 1.6 reshape.256
  247.0 2.2 reduce_sum.38
  249.3 1.6 fusion.55
  (30 shorter events, 0.4 us)
Async XLA Ops:
  0.6 16.6 %copy-start = (bf16[1024,768]{1,0:T(8,128)(2,1)S(1)}, bf16[1024,768]{1,0:T(8,128)(2,1)}, u32[]{:S(2)}) copy-start(bf16[1024,768]{1,0:T(8,128)(2,1)} %param.8) | copy-start | bytes 4718596
  136.6 7.8 %slice-start = ((s8[4718592]{0:T(1024)(128)(4,1)}), s8[4194304]{0:T(1024)(128)(4,1)S(1)}, s32[]{:S(2)}) async-start(s8[4718592]{0:T(1024)(128)(4,1)} %bitcast.12), calls=%async_computation | async-start | bytes 8388608
  137.2 7.3 %slice-start.1 = ((s8[4718592]{0:T(1024)(128)(4,1)}), s8[524288]{0:T(1024)(128)(4,1)S(1)}, s32[]{:S(2)}) async-start(s8[4718592]{0:T(1024)(128)(4,1)} %bitcast.12), calls=%async_computation.1 | async-start | bytes 1048576
  147.2 2.0 copy-start.4
  147.2 2.4 copy-start.5
  149.2 5.7 %copy-start.3 = (bf16[64,768]{1,0:T(8,128)(2,1)}, bf16[64,768]{1,0:T(8,128)(2,1)S(1)}, u32[]{:S(2)}) copy-start(bf16[64,768]{1,0:T(8,128)(2,1)S(1)} %multiply_convert_fusion.1) | copy-start | bytes 294916
  149.6 5.3 %copy-start.2 = (bf16[64,1024]{1,0:T(8,128)(2,1)S(1)}, bf16[64,1024]{1,0:T(8,128)(2,1)}, u32[]{:S(2)}) copy-start(bf16[64,1024]{1,0:T(8,128)(2,1)} %param.15) | copy-start | bytes 393220
  241.4 3.9 %copy-start.1 = (f32[384,1024]{1,0:T(8,128)S(1)}, f32[384,1024]{1,0:T(8,128)}, u32[]{:S(2)}) copy-start(f32[384,1024]{1,0:T(8,128)} %get-tuple-element.17) | copy-start | bytes 4718596

commit v2 on v1

v2 whole, which is shorter than its diff:
```python
import functools

import jax
import jax.numpy as jnp
from jax import lax
from jax.experimental import pallas as pl
from jax.experimental.pallas import tpu as pltpu
from jax.sharding import PartitionSpec as P

MESH = pl.DeviceIdType.MESH


def exchange_kernel(wide, count, stride, source, x_ref, o_ref, own_sem, send_sem, recv_sem):
    at_x, at_y = lax.axis_index("gx"), lax.axis_index("gy")
    if stride == 1:
        base = (at_y // count) * count
    else:
        base = lax.rem(at_y, stride)
    members = (lax.axis_size("gx") if wide else 1) * count
    me = (at_x * count if wide else 0) + (at_y - base) // stride

    def coords(peer):
        return (peer // count if wide else at_x, base + stride * lax.rem(peer, count))

    def copy(peer, slot):
        return pltpu.make_async_remote_copy(
            src_ref=source(x_ref, peer),
            dst_ref=o_ref.at[slot],
            send_sem=send_sem.at[peer],
            recv_sem=recv_sem.at[slot],
            device_id=coords(peer),
            device_id_type=MESH,
        )

    own = pltpu.make_async_copy(source(x_ref, me), o_ref.at[me], own_sem)
    own.start()
    barrier = pltpu.get_barrier_semaphore()

    @pl.loop(1, members)
    def _(k):
        peer = lax.rem(me + k, members)
        pl.semaphore_signal(barrier, inc=1, device_id=coords(peer), device_id_type=MESH)

    pl.semaphore_wait(barrier, members - 1)

    @pl.loop(1, members)
    def _(k):
        copy(lax.rem(me + k, members), me).start()

    @pl.loop(1, members)
    def _(k):
        peer = lax.rem(me + members - k, members)
        copy(peer, peer).wait_recv()

    @pl.loop(1, members)
    def _(k):
        copy(lax.rem(me + k, members), me).wait_send()

    own.wait()


def exchange(x, members, block, wide, count, stride, name, number, source=lambda ref, peer: ref.at[peer]):
    return pl.pallas_call(
        functools.partial(exchange_kernel, wide, count, stride, source),
        out_shape=jax.ShapeDtypeStruct((members, *block), x.dtype),
        in_specs=[pl.BlockSpec(memory_space=pl.ANY)],
        out_specs=pl.BlockSpec(memory_space=pl.ANY),
        scratch_shapes=[
            pltpu.SemaphoreType.DMA,
            pltpu.SemaphoreType.DMA((members,)),
            pltpu.SemaphoreType.DMA((members,)),
        ],
        compiler_params=pltpu.CompilerParams(collective_id=number, has_side_effects=True),
        name=name,
    )(x)


def one_hot(ids, size):
    return (ids[:, None] == jnp.arange(size, dtype=jnp.int32)[None, :]).astype(jnp.bfloat16)


def matmul(left, right):
    return jnp.dot(left, right, preferred_element_type=jnp.float32)


def body(features, seed_rows, hop1_ids, hop2_ids, w_self, w_neigh, bias, cotangent):
    split_x = lax.axis_size("gx")
    split_y = lax.axis_size("gy")
    devices = split_x * split_y
    rows_dev, width = features.shape
    hidden_width = w_self.shape[1]
    seeds = seed_rows.shape[0]
    fan_one = hop1_ids.shape[1]
    fan_two = hop2_ids.shape[2]
    near_total = seeds * fan_one
    far_total = near_total * fan_two
    near_cap = max(2, 3 * near_total // (2 * devices))
    far_cap = max(2, 3 * far_total // (2 * devices))
    cap = -(-(near_cap + far_cap) // 16) * 16
    lanes = -(-cap // 128) * 128
    bf16 = jnp.bfloat16

    half_y = split_y // 2
    half = split_x * half_y
    at_half = lax.axis_index("gy") // half_y
    mirror = lax.ppermute(features, "gy", [(i, (i + half_y) % split_y) for i in range(split_y)])

    ids = jnp.concatenate([hop2_ids.reshape(-1), hop1_ids.reshape(-1)])
    items = far_total + near_total
    holders = ids // rows_dev
    local = ids - holders * rows_dev
    held_y = holders % split_y
    other = (held_y // half_y != at_half).astype(jnp.int32)
    owners = other * half + (holders // split_y) * half_y + held_y % half_y
    at = jnp.arange(items, dtype=jnp.int32)
    is_near = at >= far_total
    owned = (jnp.arange(devices, dtype=jnp.int32)[:, None] == owners[None, :]).astype(bf16)
    earlier = ((at[:, None] < at[None, :]) & (is_near[:, None] == is_near[None, :])).astype(bf16)
    ranks = jnp.sum(matmul(owned, earlier) * owned.astype(jnp.float32), axis=0).astype(jnp.int32)
    place = jnp.where(is_near, far_cap, 0) + ranks
    high = (local // 128).astype(bf16)
    low = (local % 128).astype(bf16)
    split_ids = matmul(
        jnp.concatenate([owned * high[None, :], owned * low[None, :]], axis=0), one_hot(place, lanes)
    )
    request = (split_ids[:devices] * 128.0 + split_ids[devices:]).astype(jnp.int32)
    request = request.reshape(2, half, lanes).transpose(1, 0, 2)
    request = jnp.concatenate([request] * 4, axis=1)
    asked = exchange(request, half, (8, lanes), True, half_y, 1, "ask", 0)

    slots = owners * cap + place
    far_slots = slots[:far_total].reshape(near_total, fan_two)
    near_slots = slots[far_total:]
    picked = 0.0
    for side, table in enumerate((features, mirror)):
        served = matmul(one_hot(asked[:, side, :cap].reshape(-1), rows_dev), table).astype(bf16)
        served = served.reshape(half, cap, width)
        rows = exchange(served, half, (cap, width), True, half_y, 1, f"answer{side}", 1 + side)
        column = jnp.arange(half * cap, dtype=jnp.int32)[None, :] + side * half * cap
        far_pick = sum((far_slots[:, j : j + 1] == column).astype(jnp.float32) for j in range(fan_two))
        near_pick = (near_slots[:, None] == column).astype(bf16)
        pick = jnp.concatenate([near_pick, far_pick.astype(bf16)], axis=0)
        picked = picked + matmul(pick, rows.reshape(half * cap, width))
    near_rows = picked[:near_total].astype(bf16)
    pooled_far = (picked[near_total:] / fan_two).astype(bf16)
    seed_x = matmul(one_hot(seed_rows, rows_dev), features).astype(bf16)
    summed_near = jnp.sum(near_rows.astype(jnp.float32).reshape(seeds, fan_one, width), axis=1)
    pooled_near = (summed_near / fan_one).astype(bf16)

    x = jnp.concatenate(
        [
            jnp.concatenate([seed_x, near_rows], axis=0),
            jnp.concatenate([pooled_near, pooled_far], axis=0),
        ],
        axis=1,
    )
    pre = matmul(x, jnp.concatenate([w_self, w_neigh], axis=0)) + bias
    hidden = jnp.maximum(pre, 0.0).astype(bf16).astype(jnp.float32)
    summed = hidden[:seeds] + jnp.sum(hidden[seeds:].reshape(seeds, fan_one, hidden_width), axis=1)
    embedded = (summed / (1 + fan_one)).astype(bf16)
    spread = (cotangent.astype(jnp.float32) / (1 + fan_one)).astype(bf16)
    spread = jnp.concatenate([spread, jnp.repeat(spread, fan_one, axis=0)], axis=0)
    delta = jnp.where(pre > 0, spread, jnp.zeros((), bf16))

    ones = jnp.ones((x.shape[0], 128), bf16)
    shares = lax.dot_general(
        delta,
        jnp.concatenate([x, ones], axis=1),
        (((0,), (0,)), ((), ())),
        preferred_element_type=jnp.float32,
    ).astype(bf16)
    block = hidden_width // devices
    pair = 2
    depth = split_y // pair
    plane = split_x * pair
    shares = exchange(
        shares.reshape(split_x, depth, pair, block, -1),
        plane,
        (depth, block, shares.shape[1]),
        True,
        pair,
        1,
        "share",
        3,
        lambda ref, peer: ref.at[peer // pair, :, lax.rem(peer, pair)],
    )
    shares = jnp.sum(shares.astype(jnp.float32), axis=0).astype(bf16)
    shares = exchange(shares, depth, shares.shape[1:], False, depth, pair, "share_along", 4)
    total = jnp.sum(shares.astype(jnp.float32), axis=0)
    return (
        embedded,
        total[:, :width].T,
        total[:, width : 2 * width].T,
        total[:, 2 * width],
    )


def solution(mesh):
    in_specs = (
        P(("gx", "gy"), None),
        P(("gx", "gy")),
        P(("gx", "gy"), None),
        P(("gx", "gy"), None, None),
        P(),
        P(),
        P(),
        P(("gx", "gy"), None),
    )
    out_specs = (
        P(("gx", "gy"), None),
        P(None, ("gx", "gy")),
        P(None, ("gx", "gy")),
        P(("gx", "gy")),
    )
    return jax.shard_map(body, mesh=mesh, in_specs=in_specs, out_specs=out_specs, check_vma=False)
```

time: 251 us -> 221 us (0.88)
  Pallas kernels: 202 us -> 170 us
  other arithmetic: 7.4 us -> 11.9 us
  matrix products: 30.9 us -> 27.3 us
  local copies, waits for them, and re-layouts: 9.67 us -> 6.41 us
    pallas_call x3 -> x5, Pallas kernels: 202 us -> 170 us  [exchange(): pl.pallas_call(functools.partial(exchange_kernel, wide, count, stride, so...]
    reduce_sum x0 -> x1, other arithmetic: none -> 3.31 us  [body(): shares = jnp.sum(shares.astype(jnp.float32), axis=0).astype(bf16)]
    convert_element_type x0 -> x3, other arithmetic: none -> 3.21 us  [the longest x1 2.49 us: body(): pick = jnp.concatenate([near_pick, far_pick.astype(bf16)], axis=0)]
    dot_general x7 -> x8, matrix products: 25.4 us -> 23.5 us  [matmul(): return jnp.dot(left, right, preferred_element_type=jnp.float32)]
  transfers between devices with their start and end apart: 0 -> 1, of which waited for: 0 -> 0; matrix products, arithmetic and copies ran while one was open for 0% -> 9% of each run, Pallas kernels for 0% -> 37%
where the time goes in v2:
time: 221 us; the launch traced here: 219 us
  Pallas kernels  170 us (77%)
  matrix products  27.3 us (12%)
  other arithmetic  11.9 us (5%)
  local copies, waits for them, and re-layouts  6.41 us (3%)
  starting transfers between devices  2.37 us (1%)
    pallas_call x5, Pallas kernels, exchange(): pl.pallas_call(functools.partial(exchange_kernel, wide, count, stride, so...  170 us
    dot_general x8, matrix products, matmul(): return jnp.dot(left, right, preferred_element_type=jnp.float32)  23.5 us
  transfers between devices with their start and end apart: 1, of which 0 were waited for; matrix products, arithmetic and copies ran while one was open for 9% of the time, Pallas kernels for 37%

profile of v2, /device:TPU:11, one launch (start us, length us, event | category | flops | bytes accessed | tf_op | source)
XLA Modules:
  0.0 219.1 jit_solution(8677566754809195281)
XLA Ops:
  0.6 2.4 %collective-permute-start = (bf16[1024,768]{1,0:T(8,128)(2,1)}, bf16[1024,768]{1,0:T(8,128)(2,1)}, u32[]{:S(2)}, u32[]{:S(2)}) collective-permute-start(bf16[1024,768]{1,0:T(8,128)(2,1)} %param.8), channel_id=1, source_target_pairs={{0,4},{1,5},{2,6},{3,7},{4,0},{5,1},{6,2},{7,3},{8,12},{9,13},{10,... | collective-permute-start | bytes 4718600 | tf_op jit(solution)/shard_map/ppermute | solution.py:106
  3.0 0.9 copy.12
  4.1 0.8 copy.13
  5.4 1.8 fusion.45
  7.4 0.5 fusion.73
  8.0 0.5 slice_reduce_fusion.4
  8.6 0.5 fusion.49
  9.1 0.7 pad_add_fusion.x_ref
  9.8 30.7 %ask.1 = s32[16,8,128]{2,1,0:T(8,128)} custom-call(s32[16,8,128]{2,1,0:T(8,128)} %pad_add_fusion.x_ref), custom_call_target="tpu_custom_call" | custom-call | tf_op jit(solution)/shard_map/ask/pallas_call | solution.py:63
  40.5 1.0 slice_reduce_fusion.6
  41.5 4.2 %fusion.8 = bf16[1536,768]{1,0:T(8,128)(2,1)} fusion(bf16[1024,768]{1,0:T(8,128)(2,1)S(1)} %copy-done.1, s32[1536]{0:T(1024)S(1)} %eq.275), kind=kOutput, calls=%fused_computation.11 | convolution fusion | flops 2418671616 | bytes 3938304 | tf_op jit(solution)/shard_map/dot_general | solution.py:83
  45.7 49.8 %answer0.1 = bf16[16,96,768]{2,1,0:T(8,128)(2,1)} custom-call(bf16[16,96,768]{2,1,0:T(8,128)(2,1)} %bitcast.22), custom_call_target="tpu_custom_call" | custom-call | tf_op jit(solution)/shard_map/answer0/pallas_call | solution.py:63
  95.6 1.1 convolution_convert_fusion.1
  96.9 0.3 reshape.331
  97.2 0.6 compare_convert_fusion
  97.8 2.5 %add_convert_fusion = (bf16[320,1536]{1,0:T(8,128)(2,1)S(1)}, bf16[320,1536]{1,0:T(8,128)(2,1)S(1)}) fusion(s32[1536]{0:T(1024)S(1)} %iota_add_fusion, s32[320]{0:T(512)S(1)} %get-tuple-element.5, s32[320]{0:T(512)S(1)} %get-tuple-element.6, s32[320]{0:T(512)S(1)} %get-tuple-element.7, s32[320]{0:T(512)S(1)} %get-tuple-element.8, s32[320]{0:T(512)S(1)} %get-tuple-element.4), kind=kLoop, calls=%fused_computation.27 | loop fusion | flops 14745600 | bytes 1978624 | tf_op jit(solution)/shard_map/convert_element_type | solution.py:142
  100.4 3.0 %fusion.18 = f32[640,768]{1,0:T(8,128)} fusion(bf16[1536,768]{1,0:T(8,128)(2,1)S(1)} %bitcast.19, bf16[320,1536]{1,0:T(8,128)(2,1)S(1)} %get-tuple-element.16, bf16[320,1536]{1,0:T(8,128)(2,1)S(1)} %get-tuple-element.22), kind=kOutput, calls=%fused_computation.19 | convolution fusion | flops 1513881600 | bytes 6291456 | tf_op jit(solution)/shard_map/dot_general | solution.py:83
  103.3 5.6 %fusion.7 = bf16[1536,768]{1,0:T(8,128)(2,1)} fusion(bf16[1024,768]{1,0:T(8,128)(2,1)} %collective-permute-done, s32[1536]{0:T(1024)S(1)} %eq.286), kind=kOutput, calls=%fused_computation.10 | convolution fusion | flops 2418671616 | bytes 3938304 | tf_op jit(solution)/shard_map/dot_general | solution.py:83
  109.0 37.0 %answer1.1 = bf16[16,96,768]{2,1,0:T(8,128)(2,1)} custom-call(bf16[16,96,768]{2,1,0:T(8,128)(2,1)} %bitcast.21), custom_call_target="tpu_custom_call" | custom-call | tf_op jit(solution)/shard_map/answer1/pallas_call | solution.py:63
  146.0 3.9 %fusion.27 = f32[640,768]{1,0:T(8,128)S(1)} fusion(f32[640,768]{1,0:T(8,128)} %fusion.18, bf16[1536,768]{1,0:T(8,128)(2,1)} %bitcast.20, bf16[320,1536]{1,0:T(8,128)(2,1)S(1)} %get-tuple-element.15, bf16[320,1536]{1,0:T(8,128)(2,1)S(1)} %get-tuple-element.21), kind=kOutput, calls=%fused_computation.39 | convolution fusion | flops 1514373120 | bytes 8257536 | tf_op jit(solution)/shard_map/dot_general | solution.py:83
  150.3 0.5 reduce_sum.49
  150.8 3.4 %fusion.50 = (f32[384,1024]{1,0:T(8,128)S(1)}, f32[384,1024]{1,0:T(8,128)S(1)}) fusion(f32[1024]{0:T(1024)S(1)} %copy-done.6, bf16[768,1024]{1,0:T(8,128)(2,1)} %param.13, bf16[768,1024]{1,0:T(8,128)(2,1)} %param.12, bf16[320,768]{1,0:T(8,128)(2,1)S(1)} %fusion.48, bf16[64,768]{1,0:T(8,128)(2,1)S(1)} %multiply_convert_fusion.1, ...), kind=kOutput, calls=%fused_computation.63 | convolution fusion | flops 1220542464 | bytes 7475200 | tf_op jit(solution)/shard_map/dot_general | solution.py:83
  154.2 3.9 %convolution_convert_fusion = bf16[1024,1664]{1,0:T(8,128)(2,1)} fusion(bf16[320,768]{1,0:T(8,128)(2,1)S(1)} %fusion.48, bf16[64,768]{1,0:T(8,128)(2,1)S(1)} %multiply_convert_fusion.1, bf16[320,768]{1,0:T(8,128)(2,1)S(1)} %slice.126, bf16[64,768]{1,0:T(8,128)(2,1)S(1)} %copy-done.4, f32[384,1024]{1,0:T(8,128)S(1)} %get-tuple-element.24, ...), kind=kOutput, calls=%fused_computation.9 | convolution fusion | flops 1319469056 | bytes 6954240 | tf_op jit(solution)/shard_map/dot_general | solution.py:166
  158.0 40.3 %share.1 = bf16[8,4,32,1664]{3,2,1,0:T(8,128)(2,1)} custom-call(bf16[4,4,2,32,1664]{4,3,2,1,0:T(8,128)(2,1)} %bitcast.18), custom_call_target="tpu_custom_call" | custom-call | tf_op jit(solution)/shard_map/share/pallas_call | solution.py:63
  198.4 3.3 %reduce_sum.51.x_ref = bf16[4,32,1664]{2,1,0:T(8,128)(2,1)} reduce(bf16[8,4,32,1664]{3,2,1,0:T(8,128)(2,1)} %share.1, bf16[]{:T(256)} %constant.129.clone.1), dimensions={0}, to_apply=%region_3.4 | reduce | flops 1490944 | bytes 3833858 | tf_op jit(solution)/shard_map/reduce_sum | solution.py:187
  201.7 12.4 %share_along.1 = bf16[4,32,1664]{2,1,0:T(8,128)(2,1)} custom-call(bf16[4,32,1664]{2,1,0:T(8,128)(2,1)} %reduce_sum.51.x_ref), custom_call_target="tpu_custom_call" | custom-call | tf_op jit(solution)/shard_map/share_along/pallas_call | solution.py:63
  214.1 1.1 convert_reduce_fusion
  215.2 0.7 slice_bitcast_fusion
  215.9 0.6 slice_reduce_fusion.5
  216.6 0.2 reshape.330
  216.8 0.7 reduce_sum.50
  217.5 1.6 fusion.60
  (40 shorter events, 1.8 us)
Async XLA Ops:
  0.6 102.7 %collective-permute-start = (bf16[1024,768]{1,0:T(8,128)(2,1)}, bf16[1024,768]{1,0:T(8,128)(2,1)}, u32[]{:S(2)}, u32[]{:S(2)}) collective-permute-start(bf16[1024,768]{1,0:T(8,128)(2,1)} %param.8), channel_id=1, source_target_pairs={{0,4},{1,5},{2,6},{3,7},{4,0},{5,1},{6,2},{7,3},{8,12},{9,13},{10,... | collective-permute-start | bytes 4718600 | tf_op jit(solution)/shard_map/ppermute | solution.py:106
  7.2 34.3 %copy-start.1 = (bf16[1024,768]{1,0:T(8,128)(2,1)S(1)}, bf16[1024,768]{1,0:T(8,128)(2,1)}, u32[]{:S(2)}) copy-start(bf16[1024,768]{1,0:T(8,128)(2,1)} %param.8) | copy-start | bytes 4718596
  45.7 49.9 %copy-start.5 = (s32[64]{0:T(128)S(1)}, s32[64]{0:T(128)}, u32[]{:S(2)}) copy-start(s32[64]{0:T(128)} %param.9) | copy-start | bytes 772
  45.7 51.0 %copy-start.3 = (bf16[64,1024]{1,0:T(8,128)(2,1)S(1)}, bf16[64,1024]{1,0:T(8,128)(2,1)}, u32[]{:S(2)}) copy-start(bf16[64,1024]{1,0:T(8,128)(2,1)} %param.15) | copy-start | bytes 393220
  97.2 3.2 %copy-start = (bf16[16,96,768]{2,1,0:T(8,128)(2,1)S(1)}, bf16[16,96,768]{2,1,0:T(8,128)(2,1)}, u32[]{:S(2)}) copy-start(bf16[16,96,768]{2,1,0:T(8,128)(2,1)} %answer0.1) | copy-start | bytes 7077892
  150.1 0.7 copy-start.6
  150.8 3.4 %copy-start.4 = (bf16[64,768]{1,0:T(8,128)(2,1)S(1)}, bf16[64,768]{1,0:T(8,128)(2,1)}, u32[]{:S(2)}) copy-start(bf16[64,768]{1,0:T(8,128)(2,1)} %convolution_convert_fusion.1) | copy-start | bytes 294916
  154.2 62.3 %copy-start.2 = (f32[384,1024]{1,0:T(8,128)}, f32[384,1024]{1,0:T(8,128)S(1)}, u32[]{:S(2)}) copy-start(f32[384,1024]{1,0:T(8,128)S(1)} %get-tuple-element.23) | copy-start | bytes 4718596

commit v3 on v2

--- a/solution.py
+++ b/solution.py
@@ -10,7 +10,7 @@
 MESH = pl.DeviceIdType.MESH
 
 
-def exchange_kernel(wide, count, stride, source, x_ref, o_ref, own_sem, send_sem, recv_sem):
+def exchange_kernel(wide, count, stride, source, keep, x_ref, o_ref, own_sem, send_sem, recv_sem):
     at_x, at_y = lax.axis_index("gx"), lax.axis_index("gy")
     if stride == 1:
         base = (at_y // count) * count
@@ -32,8 +32,9 @@
             device_id_type=MESH,
         )
 
-    own = pltpu.make_async_copy(source(x_ref, me), o_ref.at[me], own_sem)
-    own.start()
+    if keep:
+        own = pltpu.make_async_copy(source(x_ref, me), o_ref.at[me], own_sem)
+        own.start()
     barrier = pltpu.get_barrier_semaphore()
 
     @pl.loop(1, members)
@@ -45,24 +46,27 @@
 
     @pl.loop(1, members)
     def _(k):
-        copy(lax.rem(me + k, members), me).start()
+        copy(lax.rem(me + k, members), me if keep else 0).start()
 
     @pl.loop(1, members)
     def _(k):
         peer = lax.rem(me + members - k, members)
-        copy(peer, peer).wait_recv()
-
-    @pl.loop(1, members)
-    def _(k):
-        copy(lax.rem(me + k, members), me).wait_send()
-
-    own.wait()
-
-
-def exchange(x, members, block, wide, count, stride, name, number, source=lambda ref, peer: ref.at[peer]):
+        copy(peer, peer if keep else 0).wait_recv()
+
+    @pl.loop(1, members)
+    def _(k):
+        copy(lax.rem(me + k, members), me if keep else 0).wait_send()
+
+    if keep:
+        own.wait()
+
+
+def exchange(
+    x, members, block, wide, count, stride, name, number, source=lambda ref, peer: ref.at[peer], keep=True
+):
     return pl.pallas_call(
-        functools.partial(exchange_kernel, wide, count, stride, source),
-        out_shape=jax.ShapeDtypeStruct((members, *block), x.dtype),
+        functools.partial(exchange_kernel, wide, count, stride, source, keep),
+        out_shape=jax.ShapeDtypeStruct((members if keep else 1, *block), x.dtype),
         in_specs=[pl.BlockSpec(memory_space=pl.ANY)],
         out_specs=pl.BlockSpec(memory_space=pl.ANY),
         scratch_shapes=[
@@ -103,7 +107,6 @@
     half_y = split_y // 2
     half = split_x * half_y
     at_half = lax.axis_index("gy") // half_y
-    mirror = lax.ppermute(features, "gy", [(i, (i + half_y) % split_y) for i in range(split_y)])
 
     ids = jnp.concatenate([hop2_ids.reshape(-1), hop1_ids.reshape(-1)])
     items = far_total + near_total
@@ -127,6 +130,9 @@
     request = request.reshape(2, half, lanes).transpose(1, 0, 2)
     request = jnp.concatenate([request] * 4, axis=1)
     asked = exchange(request, half, (8, lanes), True, half_y, 1, "ask", 0)
+
+    asked, sent = lax.optimization_barrier((asked, features))
+    mirror = lax.ppermute(sent, "gy", [(i, (i + half_y) % split_y) for i in range(split_y)])
 
     slots = owners * cap + place
     far_slots = slots[:far_total].reshape(near_total, fan_two)
@@ -172,18 +178,23 @@
     block = hidden_width // devices
     pair = 2
     depth = split_y // pair
-    plane = split_x * pair
-    shares = exchange(
-        shares.reshape(split_x, depth, pair, block, -1),
-        plane,
-        (depth, block, shares.shape[1]),
-        True,
+    shares = shares.reshape(split_x, depth, pair, block, -1)
+    tail = (depth, block, shares.shape[-1])
+    given = exchange(
+        shares,
+        pair,
+        (split_x, *tail),
+        False,
         pair,
         1,
-        "share",
+        "share_pair",
         3,
-        lambda ref, peer: ref.at[peer // pair, :, lax.rem(peer, pair)],
-    )
+        lambda ref, peer: ref.at[:, :, peer],
+        keep=False,
+    )[0]
+    kept = lax.dynamic_index_in_dim(shares, lax.axis_index("gy") % pair, 2, keepdims=False)
+    shares = (kept.astype(jnp.float32) + given.astype(jnp.float32)).astype(bf16)
+    shares = exchange(shares, split_x, tail, True, 1, 1, "share_across", 5)
     shares = jnp.sum(shares.astype(jnp.float32), axis=0).astype(bf16)
     shares = exchange(shares, depth, shares.shape[1:], False, depth, pair, "share_along", 4)
     total = jnp.sum(shares.astype(jnp.float32), axis=0)

time: 221 us -> 205 us (0.928)
  Pallas kernels: 170 us -> 146 us
  local copies, waits for them, and re-layouts: 6.41 us -> 9.92 us
  other arithmetic: 11.9 us -> 15.1 us
    pallas_call x5 -> x6, Pallas kernels: 170 us -> 146 us  [exchange(): pl.pallas_call(functools.partial(exchange_kernel, wide, count, stride, so...]
    convert_element_type x0 -> x1, other arithmetic: none -> 3.09 us  [body(): shares = (kept.astype(jnp.float32) + given.astype(jnp.float32)).astype(bf16)]
  transfers between devices with their start and end apart: 1 -> 1, of which waited for: 0 -> 0; matrix products, arithmetic and copies ran while one was open for 9% -> 9% of each run, Pallas kernels for 37% -> 30%
where the time goes in v3:
time: 205 us; the launch traced here: 202 us
  Pallas kernels  146 us (71%)
  matrix products  28.4 us (14%)
  other arithmetic  15.1 us (7%)
  local copies, waits for them, and re-layouts  9.92 us (5%)
  starting transfers between devices  2.37 us (1%)
    pallas_call x6, Pallas kernels, exchange(): pl.pallas_call(functools.partial(exchange_kernel, wide, count, stride, so...  146 us
    dot_general x8, matrix products, matmul(): return jnp.dot(left, right, preferred_element_type=jnp.float32)  24.6 us
  transfers between devices with their start and end apart: 1, of which 0 were waited for; matrix products, arithmetic and copies ran while one was open for 9% of the time, Pallas kernels for 30%

profile of v3, /device:TPU:11, one launch (start us, length us, event | category | flops | bytes accessed | tf_op | source)
XLA Modules:
  0.0 202.4 jit_solution(12307572865226901373)
XLA Ops:
  0.7 0.9 copy.13
  1.8 0.8 copy.14
  2.8 1.8 fusion.46
  5.2 0.7 pad_add_fusion.x_ref
  5.8 6.7 %ask.1 = s32[16,8,128]{2,1,0:T(8,128)} custom-call(s32[16,8,128]{2,1,0:T(8,128)} %pad_add_fusion.x_ref), custom_call_target="tpu_custom_call" | custom-call | tf_op jit(solution)/shard_map/ask/pallas_call | solution.py:67
  12.6 2.4 %collective-permute-start = (bf16[1024,768]{1,0:T(8,128)(2,1)S(1)}, bf16[1024,768]{1,0:T(8,128)(2,1)}, u32[]{:S(2)}, u32[]{:S(2)}) collective-permute-start(bf16[1024,768]{1,0:T(8,128)(2,1)S(1)} %copy-done.2), channel_id=1, source_target_pairs={{0,4},{1,5},{2,6},{3,7},{4,0},{5,1},{6,2},{7,3},{8,12},{9,13},{10,... | collective-permute-start | bytes 4718600 | tf_op jit(solution)/shard_map/ppermute | solution.py:135
  16.0 1.1 slice_reduce_fusion.4
  17.1 1.0 slice_reduce_fusion.6
  18.1 4.2 %fusion.9 = bf16[1536,768]{1,0:T(8,128)(2,1)} fusion(bf16[1024,768]{1,0:T(8,128)(2,1)S(1)} %copy-done.2, s32[1536]{0:T(1024)S(1)} %eq.277), kind=kOutput, calls=%fused_computation.13 | convolution fusion | flops 2418671616 | bytes 3938304 | tf_op jit(solution)/shard_map/dot_general | solution.py:87
  22.3 60.5 %answer0.1 = bf16[16,96,768]{2,1,0:T(8,128)(2,1)} custom-call(bf16[16,96,768]{2,1,0:T(8,128)(2,1)} %bitcast.31), custom_call_target="tpu_custom_call" | custom-call | tf_op jit(solution)/shard_map/answer0/pallas_call | solution.py:67
  82.8 0.7 eq.288
  83.5 1.1 convolution_convert_fusion.1
  84.6 0.6 copy-done.5
  85.4 1.2 reshape.335
  87.2 0.6 compare_convert_fusion
  87.9 3.3 %add_convert_fusion = (bf16[320,1536]{1,0:T(8,128)(2,1)S(1)}, bf16[320,1536]{1,0:T(8,128)(2,1)S(1)}) fusion(s32[1536]{0:T(1024)S(1)} %iota_add_fusion, s32[320]{0:T(512)S(1)} %get-tuple-element.9, s32[320]{0:T(512)S(1)} %get-tuple-element.10, s32[320]{0:T(512)S(1)} %get-tuple-element.11, s32[320]{0:T(512)} %get-tuple-element.12, s32[320]{0:T(512)S(1)} %get-tuple-element.8), kind=kLoop, calls=%fused_computation.29 | loop fusion | flops 14745600 | bytes 1978624 | tf_op jit(solution)/shard_map/convert_element_type | solution.py:148
  91.2 3.0 %fusion.19 = f32[640,768]{1,0:T(8,128)} fusion(bf16[1536,768]{1,0:T(8,128)(2,1)S(1)} %bitcast.28, bf16[320,1536]{1,0:T(8,128)(2,1)S(1)} %get-tuple-element.20, bf16[320,1536]{1,0:T(8,128)(2,1)S(1)} %get-tuple-element.26), kind=kOutput, calls=%fused_computation.21 | convolution fusion | flops 1513881600 | bytes 6291456 | tf_op jit(solution)/shard_map/dot_general | solution.py:87
  94.2 5.6 %fusion.8 = bf16[1536,768]{1,0:T(8,128)(2,1)} fusion(bf16[1024,768]{1,0:T(8,128)(2,1)} %collective-permute-done, s32[1536]{0:T(1024)S(1)} %copy-done.9), kind=kOutput, calls=%fused_computation.12 | convolution fusion | flops 2418671616 | bytes 3938304 | tf_op jit(solution)/shard_map/dot_general | solution.py:87
  99.8 41.3 %answer1.1 = bf16[16,96,768]{2,1,0:T(8,128)(2,1)} custom-call(bf16[16,96,768]{2,1,0:T(8,128)(2,1)} %bitcast.30), custom_call_target="tpu_custom_call" | custom-call | tf_op jit(solution)/shard_map/answer1/pallas_call | solution.py:67
  141.1 3.9 %fusion.28 = f32[640,768]{1,0:T(8,128)S(1)} fusion(f32[640,768]{1,0:T(8,128)} %fusion.19, bf16[1536,768]{1,0:T(8,128)(2,1)} %bitcast.29, bf16[320,1536]{1,0:T(8,128)(2,1)S(1)} %get-tuple-element.19, bf16[320,1536]{1,0:T(8,128)(2,1)S(1)} %get-tuple-element.25), kind=kOutput, calls=%fused_computation.41 | convolution fusion | flops 1514373120 | bytes 8257536 | tf_op jit(solution)/shard_map/dot_general | solution.py:87
  146.2 4.5 %fusion.51 = (f32[384,1024]{1,0:T(8,128)}, f32[384,1024]{1,0:T(8,128)S(1)}) fusion(f32[1024]{0:T(1024)S(1)} %copy-done.12, bf16[768,1024]{1,0:T(8,128)(2,1)} %param.13, bf16[768,1024]{1,0:T(8,128)(2,1)} %param.12, bf16[320,768]{1,0:T(8,128)(2,1)S(1)} %fusion.49, bf16[64,768]{1,0:T(8,128)(2,1)S(1)} %multiply_convert_fusion.1, ...), kind=kOutput, calls=%fused_computation.65 | convolution fusion | flops 1220542464 | bytes 7475200 | tf_op jit(solution)/shard_map/dot_general | solution.py:87
  150.7 3.8 %convolution_convert_fusion = bf16[1024,1664]{1,0:T(8,128)(2,1)} fusion(bf16[320,768]{1,0:T(8,128)(2,1)S(1)} %fusion.49, bf16[64,768]{1,0:T(8,128)(2,1)S(1)} %multiply_convert_fusion.1, bf16[320,768]{1,0:T(8,128)(2,1)S(1)} %slice.126, bf16[64,768]{1,0:T(8,128)(2,1)S(1)} %copy-done.8, f32[384,1024]{1,0:T(8,128)S(1)} %get-tuple-element.28, ...), kind=kOutput, calls=%fused_computation.9 | convolution fusion | flops 1319469056 | bytes 6954240 | tf_op jit(solution)/shard_map/dot_general | solution.py:172
  154.5 4.0 %share_pair.1 = bf16[1,4,4,32,1664]{4,3,2,1,0:T(8,128)(2,1)} custom-call(bf16[4,4,2,32,1664]{4,3,2,1,0:T(8,128)(2,1)} %bitcast.26), custom_call_target="tpu_custom_call" | custom-call | tf_op jit(solution)/shard_map/share_pair/pallas_call | solution.py:67
  158.5 3.1 %fusion.7.x_ref = bf16[4,4,32,1664]{3,2,1,0:T(8,128)(2,1)} fusion(bf16[1,4,4,32,1664]{4,3,2,1,0:T(8,128)(2,1)} %share_pair.1, bf16[4,4,2,32,1664]{4,3,2,1,0:T(8,128)(2,1)S(1)} %bitcast.27, s32[]{:T(128)S(6)} %select_n.124), kind=kLoop, calls=%fused_computation.11 | loop fusion | flops 3407872 | bytes 5111812 | tf_op jit(solution)/shard_map/convert_element_type | solution.py:196
  161.6 21.7 %share_across.1 = bf16[4,4,32,1664]{3,2,1,0:T(8,128)(2,1)} custom-call(bf16[4,4,32,1664]{3,2,1,0:T(8,128)(2,1)} %fusion.7.x_ref), custom_call_target="tpu_custom_call" | custom-call | tf_op jit(solution)/shard_map/share_across/pallas_call | solution.py:67
  183.3 2.7 %reduce_sum.51.x_ref = bf16[4,32,1664]{2,1,0:T(8,128)(2,1)} reduce(bf16[4,4,32,1664]{3,2,1,0:T(8,128)(2,1)} %share_across.1, bf16[]{:T(256)} %constant.143.clone.1), dimensions={0}, to_apply=%region_3.4 | reduce | flops 638976 | bytes 2129922 | tf_op jit(solution)/shard_map/reduce_sum | solution.py:198
  186.0 11.3 %share_along.1 = bf16[4,32,1664]{2,1,0:T(8,128)(2,1)} custom-call(bf16[4,32,1664]{2,1,0:T(8,128)(2,1)} %reduce_sum.51.x_ref), custom_call_target="tpu_custom_call" | custom-call | tf_op jit(solution)/shard_map/share_along/pallas_call | solution.py:67
  197.3 1.1 convert_reduce_fusion
  198.4 0.7 slice_bitcast_fusion
  199.1 0.6 slice_reduce_fusion.5
  200.1 0.7 reduce_sum.50
  200.7 1.6 fusion.61
  (54 shorter events, 4.2 us)
Async XLA Ops:
  2.8 9.7 %copy-start.2 = (bf16[1024,768]{1,0:T(8,128)(2,1)S(1)}, bf16[1024,768]{1,0:T(8,128)(2,1)}, u32[]{:S(2)}) copy-start(bf16[1024,768]{1,0:T(8,128)(2,1)} %param.8) | copy-start | bytes 4718596
  12.6 81.6 %collective-permute-start = (bf16[1024,768]{1,0:T(8,128)(2,1)S(1)}, bf16[1024,768]{1,0:T(8,128)(2,1)}, u32[]{:S(2)}, u32[]{:S(2)}) collective-permute-start(bf16[1024,768]{1,0:T(8,128)(2,1)S(1)} %copy-done.2), channel_id=1, source_target_pairs={{0,4},{1,5},{2,6},{3,7},{4,0},{5,1},{6,2},{7,3},{8,12},{9,13},{10,... | collective-permute-start | bytes 4718600 | tf_op jit(solution)/shard_map/ppermute | solution.py:135
  22.3 61.2 %copy-start.11 = (s32[64]{0:T(128)S(1)}, s32[64]{0:T(128)}, u32[]{:S(2)}) copy-start(s32[64]{0:T(128)} %param.9) | copy-start | bytes 772
  22.3 62.3 %copy-start.7 = (bf16[64,1024]{1,0:T(8,128)(2,1)S(1)}, bf16[64,1024]{1,0:T(8,128)(2,1)}, u32[]{:S(2)}) copy-start(bf16[64,1024]{1,0:T(8,128)(2,1)} %param.15) | copy-start | bytes 393220
  84.6 0.7 copy-start.5
  87.2 3.9 %copy-start.1 = (bf16[16,96,768]{2,1,0:T(8,128)(2,1)S(1)}, bf16[16,96,768]{2,1,0:T(8,128)(2,1)}, u32[]{:S(2)}) copy-start(bf16[16,96,768]{2,1,0:T(8,128)(2,1)} %answer0.1) | copy-start | bytes 7077892
  91.2 3.0 %copy-start.9 = (s32[1536]{0:T(1024)S(1)}, s32[1536]{0:T(1024)}, u32[]{:S(2)}) copy-start(s32[1536]{0:T(1024)} %eq.288) | copy-start | bytes 18436
  145.2 0.9 copy-start.8
  145.3 0.9 copy-start.12
  146.1 4.5 %copy-start.4 = (bf16[320,1024]{1,0:T(8,128)(2,1)S(1)}, bf16[320,1024]{1,0:T(8,128)(2,1)}, u32[]{:S(2)}) copy-start(bf16[320,1024]{1,0:T(8,128)(2,1)} %reshape.335) | copy-start | bytes 1966084
  146.1 4.5 %copy-start.6 = (bf16[64,1024]{1,0:T(8,128)(2,1)S(1)}, bf16[64,1024]{1,0:T(8,128)(2,1)}, u32[]{:S(2)}) copy-start(bf16[64,1024]{1,0:T(8,128)(2,1)} %copy-done.5) | copy-start | bytes 393220
  146.1 4.5 %copy-start.10 = (bf16[1664]{0:T(1024)(128)(2,1)S(1)}, bf16[1664]{0:T(1024)(128)(2,1)}, u32[]{:S(2)}) copy-start(bf16[1664]{0:T(1024)(128)(2,1)} %pad.4.clone) | copy-start | bytes 9988
  154.5 4.0 %copy-start = (bf16[1024,1664]{1,0:T(8,128)(2,1)S(1)}, bf16[1024,1664]{1,0:T(8,128)(2,1)}, u32[]{:S(2)}) copy-start(bf16[1024,1664]{1,0:T(8,128)(2,1)} %convolution_convert_fusion) | copy-start | bytes 10223620
  183.3 16.4 %copy-start.3 = (f32[384,1024]{1,0:T(8,128)S(1)}, f32[384,1024]{1,0:T(8,128)}, u32[]{:S(2)}) copy-start(f32[384,1024]{1,0:T(8,128)} %get-tuple-element.27) | copy-start | bytes 4718596

commit v4 on v3

--- a/solution.py
+++ b/solution.py
@@ -6,6 +6,7 @@
 from jax.experimental import pallas as pl
 from jax.experimental.pallas import tpu as pltpu
 from jax.sharding import PartitionSpec as P
+
 
 MESH = pl.DeviceIdType.MESH
 
@@ -62,7 +63,7 @@
 
 
 def exchange(
-    x, members, block, wide, count, stride, name, number, source=lambda ref, peer: ref.at[peer], keep=True
+    x, members, block, wide, count, stride, number, source=lambda ref, peer: ref.at[peer], keep=True
 ):
     return pl.pallas_call(
         functools.partial(exchange_kernel, wide, count, stride, source, keep),
@@ -75,7 +76,6 @@
             pltpu.SemaphoreType.DMA((members,)),
         ],
         compiler_params=pltpu.CompilerParams(collective_id=number, has_side_effects=True),
-        name=name,
     )(x)
 
 
@@ -129,24 +129,40 @@
     request = (split_ids[:devices] * 128.0 + split_ids[devices:]).astype(jnp.int32)
     request = request.reshape(2, half, lanes).transpose(1, 0, 2)
     request = jnp.concatenate([request] * 4, axis=1)
-    asked = exchange(request, half, (8, lanes), True, half_y, 1, "ask", 0)
-
-    asked, sent = lax.optimization_barrier((asked, features))
-    mirror = lax.ppermute(sent, "gy", [(i, (i + half_y) % split_y) for i in range(split_y)])
+    asked = exchange(request, half, (8, lanes), True, half_y, 1, 0)
+
+    first = max(128, 2 * width // 3 // 128 * 128)
+    over = [(i, (i + half_y) % split_y) for i in range(split_y)]
+    asked, sent = lax.optimization_barrier((asked, features[:, :first]))
+    mirror_first = lax.ppermute(sent, "gy", over)
 
     slots = owners * cap + place
     far_slots = slots[:far_total].reshape(near_total, fan_two)
     near_slots = slots[far_total:]
-    picked = 0.0
-    for side, table in enumerate((features, mirror)):
-        served = matmul(one_hot(asked[:, side, :cap].reshape(-1), rows_dev), table).astype(bf16)
-        served = served.reshape(half, cap, width)
-        rows = exchange(served, half, (cap, width), True, half_y, 1, f"answer{side}", 1 + side)
+
+    def pick(side):
         column = jnp.arange(half * cap, dtype=jnp.int32)[None, :] + side * half * cap
         far_pick = sum((far_slots[:, j : j + 1] == column).astype(jnp.float32) for j in range(fan_two))
         near_pick = (near_slots[:, None] == column).astype(bf16)
-        pick = jnp.concatenate([near_pick, far_pick.astype(bf16)], axis=0)
-        picked = picked + matmul(pick, rows.reshape(half * cap, width))
+        return jnp.concatenate([near_pick, far_pick.astype(bf16)], axis=0)
+
+    def answer(asked, side, table, number):
+        columns = table.shape[1]
+        served = matmul(one_hot(asked[:, side, :cap].reshape(-1), rows_dev), table).astype(bf16)
+        rows = exchange(
+            served.reshape(half, cap, columns), half, (cap, columns), True, half_y, 1, number
+        )
+        return rows.reshape(half * cap, columns)
+
+    rows_own = answer(asked, 0, features, 1)
+    rows_own, sent = lax.optimization_barrier((rows_own, features[:, first:]))
+    mirror_last = lax.ppermute(sent, "gy", over)
+    rows_first = answer(asked, 1, mirror_first, 2)
+    rows_first, asked = lax.optimization_barrier((rows_first, asked))
+    rows_last = answer(asked, 1, mirror_last, 6)
+    picked = matmul(pick(0), rows_own) + jnp.concatenate(
+        [matmul(pick(1), rows_first), matmul(pick(1), rows_last)], axis=1
+    )
     near_rows = picked[:near_total].astype(bf16)
     pooled_far = (picked[near_total:] / fan_two).astype(bf16)
     seed_x = matmul(one_hot(seed_rows, rows_dev), features).astype(bf16)
@@ -187,16 +203,15 @@
         False,
         pair,
         1,
-        "share_pair",
         3,
         lambda ref, peer: ref.at[:, :, peer],
         keep=False,
     )[0]
     kept = lax.dynamic_index_in_dim(shares, lax.axis_index("gy") % pair, 2, keepdims=False)
     shares = (kept.astype(jnp.float32) + given.astype(jnp.float32)).astype(bf16)
-    shares = exchange(shares, split_x, tail, True, 1, 1, "share_across", 5)
+    shares = exchange(shares, split_x, tail, True, 1, 1, 5)
     shares = jnp.sum(shares.astype(jnp.float32), axis=0).astype(bf16)
-    shares = exchange(shares, depth, shares.shape[1:], False, depth, pair, "share_along", 4)
+    shares = exchange(shares, depth, shares.shape[1:], False, depth, pair, 4)
     total = jnp.sum(shares.astype(jnp.float32), axis=0)
     return (
         embedded,
@@ -223,4 +238,5 @@
         P(None, ("gx", "gy")),
         P(("gx", "gy")),
     )
+
     return jax.shard_map(body, mesh=mesh, in_specs=in_specs, out_specs=out_specs, check_vma=False)

time: 205 us -> 236 us (1.15)
  waiting for transfers between devices: 0.01 us -> 56.7 us
  Pallas kernels: 146 us -> 120 us
    ppermute x1 -> x2, waiting for transfers between devices: 0.01 us -> 56.7 us  [the longest x1 56.7 us: body(): mirror_first = lax.ppermute(sent, 'gy', over)]
    pallas_call x6 -> x7, Pallas kernels: 146 us -> 120 us  [exchange(): pl.pallas_call(functools.partial(exchange_kernel, wide, count, stride, so...]
    slice x2 -> x5, local copies, waits for them, and re-layouts: 2.07 us -> 4.6 us  [the longest x2 1.83 us: answer(): asked[:, side, :cap].reshape(-1)]
    dot_general x8 -> x10, matrix products: 24.6 us -> 23.9 us  [matmul(): return jnp.dot(left, right, preferred_element_type=jnp.float32)]
  transfers between devices with their start and end apart: 1 -> 2, of which waited for: 0 -> 1; matrix products, arithmetic and copies ran while one was open for 9% -> 6% of each run, Pallas kernels for 30% -> 11%
where the time goes in v4:
time: 236 us; the launch traced here: 235 us
  Pallas kernels  120 us (51%)
  waiting for transfers between devices  56.7 us (24%)
  matrix products  27.7 us (12%)
  other arithmetic  17.3 us (7%)
  local copies, waits for them, and re-layouts  9.47 us (4%)
  starting transfers between devices  2.45 us (1%)
    pallas_call x7, Pallas kernels, exchange(): pl.pallas_call(functools.partial(exchange_kernel, wide, count, stride, so...  120 us
    ppermute x1, waiting for transfers between devices, body(): mirror_first = lax.ppermute(sent, 'gy', over)  56.7 us
    dot_general x10, matrix products, matmul(): return jnp.dot(left, right, preferred_element_type=jnp.float32)  23.9 us
  transfers between devices with their start and end apart: 2, of which 1 were waited for; matrix products, arithmetic and copies ran while one was open for 6% of the time, Pallas kernels for 11%

profile of v4, /device:TPU:11, one launch (start us, length us, event | category | flops | bytes accessed | tf_op | source)
XLA Modules:
  0.0 235.1 jit_solution(4448779928660225366)
XLA Ops:
  0.7 1.4 slice.86
  2.4 0.8 slice.88
  4.0 1.8 fusion.46
  6.3 0.7 pad_add_fusion.x_ref
  7.0 6.7 %shard_map.111 = s32[16,8,128]{2,1,0:T(8,128)} custom-call(s32[16,8,128]{2,1,0:T(8,128)} %pad_add_fusion.x_ref), custom_call_target="tpu_custom_call" | custom-call | tf_op jit(solution)/shard_map/pallas_call | solution.py:68
  13.7 1.0 slice_reduce_fusion.7
  14.7 4.2 %fusion.9 = bf16[1536,768]{1,0:T(8,128)(2,1)} fusion(bf16[1024,768]{1,0:T(8,128)(2,1)S(1)} %copy-done.1, s32[1536]{0:T(1024)S(1)} %eq.158), kind=kOutput, calls=%fused_computation.14 | convolution fusion | flops 2418671616 | bytes 3938304 | tf_op jit(solution)/shard_map/dot_general | solution.py:87
  18.9 35.0 %shard_map.112 = bf16[16,96,768]{2,1,0:T(8,128)(2,1)} custom-call(bf16[16,96,768]{2,1,0:T(8,128)(2,1)} %bitcast.33), custom_call_target="tpu_custom_call" | custom-call | tf_op jit(solution)/shard_map/pallas_call | solution.py:68
  53.9 2.4 %collective-permute-start.1 = (bf16[1024,256]{1,0:T(8,128)(2,1)}, bf16[1024,256]{1,0:T(8,128)(2,1)}, u32[]{:S(2)}, u32[]{:S(2)}) collective-permute-start(bf16[1024,256]{1,0:T(8,128)(2,1)} %slice.88), channel_id=1, source_target_pairs={{0,4},{1,5},{2,6},{3,7},{4,0},{5,1},{6,2},{7,3},{8,12},{9,13},{10,... | collective-permute-start | bytes 1572872 | tf_op jit(solution)/shard_map/ppermute | solution.py:159
  57.4 1.9 fusion.26
  60.3 3.4 %add_convert_fusion.1 = (bf16[320,1536]{1,0:T(8,128)(2,1)}, bf16[320,1536]{1,0:T(8,128)(2,1)}) fusion(s32[320]{0:T(512)S(1)} %get-tuple-element.17, s32[320]{0:T(512)S(1)} %get-tuple-element.18, s32[320]{0:T(512)S(1)} %get-tuple-element.19, s32[320]{0:T(512)S(1)} %get-tuple-element.20, s32[320]{0:T(512)S(1)} %get-tuple-element.16, s32[1536]{0:T(1024)S(1)} %iota_add_fusion), kind=kLoop, calls=%fused_computation.32 | loop fusion | flops 14745600 | bytes 1978624 | tf_op jit(solution)/shard_map/convert_element_type | solution.py:147
  64.3 56.7 %collective-permute-done = bf16[1024,512]{1,0:T(8,128)(2,1)} collective-permute-done((bf16[1024,512]{1,0:T(8,128)(2,1)S(1)}, bf16[1024,512]{1,0:T(8,128)(2,1)}, u32[]{:S(2)}, u32[]{:S(2)}) %collective-permute-start) | collective-permute-done | bytes 1048608 | tf_op jit(solution)/shard_map/ppermute | solution.py:137
  121.1 4.3 %fusion.17 = bf16[1536,512]{1,0:T(8,128)(2,1)} fusion(bf16[1024,512]{1,0:T(8,128)(2,1)} %collective-permute-done, s32[1536]{0:T(1024)S(1)} %eq.169), kind=kOutput, calls=%fused_computation.22 | convolution fusion | flops 1612972032 | bytes 2627584 | tf_op jit(solution)/shard_map/dot_general | solution.py:87
  125.3 26.2 %shard_map.113 = bf16[16,96,512]{2,1,0:T(8,128)(2,1)} custom-call(bf16[16,96,512]{2,1,0:T(8,128)(2,1)} %bitcast.35), custom_call_target="tpu_custom_call" | custom-call | tf_op jit(solution)/shard_map/pallas_call | solution.py:68
  151.5 0.9 slice_reduce_fusion.6
  152.5 3.3 %fusion.18 = bf16[1536,256]{1,0:T(8,128)(2,1)} fusion(bf16[1024,256]{1,0:T(8,128)(2,1)} %collective-permute-done.1, s32[1536]{0:T(1024)S(1)} %eq.173), kind=kOutput, calls=%fused_computation.23 | convolution fusion | flops 807272448 | bytes 1316864 | tf_op jit(solution)/shard_map/dot_general | solution.py:87
  155.8 13.7 %shard_map.114 = bf16[16,96,256]{2,1,0:T(8,128)(2,1)} custom-call(bf16[16,96,256]{2,1,0:T(8,128)(2,1)} %bitcast.36), custom_call_target="tpu_custom_call" | custom-call | tf_op jit(solution)/shard_map/pallas_call | solution.py:68
  169.6 1.9 fusion.37
  171.5 1.2 fusion.38
  173.7 1.7 maximum_add_fusion
  175.4 0.8 fusion.49
  177.0 4.7 %fusion.51 = (f32[384,1024]{1,0:T(8,128)}, f32[384,1024]{1,0:T(8,128)S(1)}) fusion(f32[1024]{0:T(1024)S(1)} %copy-done.14, bf16[768,1024]{1,0:T(8,128)(2,1)} %param.13, bf16[768,1024]{1,0:T(8,128)(2,1)} %param.12, bf16[320,768]{1,0:T(8,128)(2,1)} %fusion.49, bf16[64,768]{1,0:T(8,128)(2,1)S(1)} %multiply_convert_fusion.1, bf16[320,768]{1,0:T(8,128)(2,1)S(1)} %slice.144, ...), kind=kOutput, calls=%fused_computation.68 | convolution fusion | flops 1220542464 | bytes 7475200 | tf_op jit(solution)/shard_map/dot_general | solution.py:87
  181.7 3.8 %convolution_convert_fusion = bf16[1024,1664]{1,0:T(8,128)(2,1)} fusion(bf16[320,768]{1,0:T(8,128)(2,1)S(1)} %copy-done.9, bf16[64,768]{1,0:T(8,128)(2,1)S(1)} %multiply_convert_fusion.1, bf16[320,768]{1,0:T(8,128)(2,1)S(1)} %slice.144, bf16[64,768]{1,0:T(8,128)(2,1)S(1)} %convolution_convert_fusion.1, f32[384,1024]{1,0:T(8,128)S(1)} %get-tuple-element.36, ...), kind=kOutput, calls=%fused_computation.11 | convolution fusion | flops 1319469056 | bytes 6954240 | tf_op jit(solution)/shard_map/dot_general | solution.py:188
  185.5 4.0 %shard_map.115 = bf16[1,4,4,32,1664]{4,3,2,1,0:T(8,128)(2,1)} custom-call(bf16[4,4,2,32,1664]{4,3,2,1,0:T(8,128)(2,1)} %bitcast.30), custom_call_target="tpu_custom_call" | custom-call | tf_op jit(solution)/shard_map/pallas_call | solution.py:68
  189.5 3.1 %fusion.8.x_ref = bf16[4,4,32,1664]{3,2,1,0:T(8,128)(2,1)} fusion(bf16[1,4,4,32,1664]{4,3,2,1,0:T(8,128)(2,1)} %shard_map.115, bf16[4,4,2,32,1664]{4,3,2,1,0:T(8,128)(2,1)S(1)} %bitcast.31, s32[]{:T(128)S(6)} %select_n.124), kind=kLoop, calls=%fused_computation.13 | loop fusion | flops 3407872 | bytes 5111812 | tf_op jit(solution)/shard_map/convert_element_type | solution.py:211
  192.6 21.6 %shard_map.116 = bf16[4,4,32,1664]{3,2,1,0:T(8,128)(2,1)} custom-call(bf16[4,4,32,1664]{3,2,1,0:T(8,128)(2,1)} %fusion.8.x_ref), custom_call_target="tpu_custom_call" | custom-call | tf_op jit(solution)/shard_map/pallas_call | solution.py:68
  214.2 2.7 %reduce_sum.51.x_ref = bf16[4,32,1664]{2,1,0:T(8,128)(2,1)} reduce(bf16[4,4,32,1664]{3,2,1,0:T(8,128)(2,1)} %shard_map.116, bf16[]{:T(256)} %constant.143.clone.1), dimensions={0}, to_apply=%region_3.4 | reduce | flops 638976 | bytes 2129922 | tf_op jit(solution)/shard_map/reduce_sum | solution.py:213
  216.9 13.1 %shard_map.117 = bf16[4,32,1664]{2,1,0:T(8,128)(2,1)} custom-call(bf16[4,32,1664]{2,1,0:T(8,128)(2,1)} %reduce_sum.51.x_ref), custom_call_target="tpu_custom_call" | custom-call | tf_op jit(solution)/shard_map/pallas_call | solution.py:68
  230.0 1.1 convert_reduce_fusion
  231.1 0.7 slice_bitcast_fusion
  232.8 0.7 reduce_sum.50
  233.4 1.6 fusion.61
  (67 shorter events, 7.0 us)
Async XLA Ops:
  0.6 1.7 copy-start.1
  0.6 2.5 %copy-start.12 = (s32[64,5]{0,1:T(8,128)S(1)}, s32[64,5]{0,1:T(8,128)}, u32[]{:S(2)}) copy-start(s32[64,5]{0,1:T(8,128)} %param.10) | copy-start | bytes 3844
  0.7 2.8 %copy-start.11 = (s32[64,5,5]{0,2,1:T(8,128)S(1)}, s32[64,5,5]{0,2,1:T(8,128)}, u32[]{:S(2)}) copy-start(s32[64,5,5]{0,2,1:T(8,128)} %param.11) | copy-start | bytes 19204
  53.9 6.0 %copy-start.13 = (s32[64]{0:T(128)S(1)}, s32[64]{0:T(128)}, u32[]{:S(2)}) copy-start(s32[64]{0:T(128)} %param.9) | copy-start | bytes 772
  53.9 98.6 %collective-permute-start.1 = (bf16[1024,256]{1,0:T(8,128)(2,1)}, bf16[1024,256]{1,0:T(8,128)(2,1)}, u32[]{:S(2)}, u32[]{:S(2)}) collective-permute-start(bf16[1024,256]{1,0:T(8,128)(2,1)} %slice.88), channel_id=1, source_target_pairs={{0,4},{1,5},{2,6},{3,7},{4,0},{5,1},{6,2},{7,3},{8,12},{9,13},{10,... | collective-permute-start | bytes 1572872 | tf_op jit(solution)/shard_map/ppermute | solution.py:159
  56.3 64.8 %collective-permute-start = (bf16[1024,512]{1,0:T(8,128)(2,1)S(1)}, bf16[1024,512]{1,0:T(8,128)(2,1)}, u32[]{:S(2)}, u32[]{:S(2)}) collective-permute-start(bf16[1024,512]{1,0:T(8,128)(2,1)S(1)} %slice.86), channel_id=1, source_target_pairs={{0,4},{1,5},{2,6},{3,7},{4,0},{5,1},{6,2},{7,3},{8,12},{9,13},{10,... | collective-permute-start | bytes 3145736 | tf_op jit(solution)/shard_map/ppermute | solution.py:137
  59.9 3.9 %copy-start.10 = (bf16[64,1024]{1,0:T(8,128)(2,1)S(1)}, bf16[64,1024]{1,0:T(8,128)(2,1)}, u32[]{:S(2)}) copy-start(bf16[64,1024]{1,0:T(8,128)(2,1)} %param.15) | copy-start | bytes 393220
  152.4 17.1 %copy-start.6 = (bf16[320,1536]{1,0:T(8,128)(2,1)S(1)}, bf16[320,1536]{1,0:T(8,128)(2,1)}, u32[]{:S(2)}) copy-start(bf16[320,1536]{1,0:T(8,128)(2,1)} %get-tuple-element.34) | copy-start | bytes 2949124
  152.4 17.1 %copy-start.8 = (bf16[320,1536]{1,0:T(8,128)(2,1)S(1)}, bf16[320,1536]{1,0:T(8,128)(2,1)}, u32[]{:S(2)}) copy-start(bf16[320,1536]{1,0:T(8,128)(2,1)} %get-tuple-element.28) | copy-start | bytes 2949124
  169.5 1.9 copy-start.4
  171.5 1.7 copy-start.2
  171.5 1.9 copy-start.5
  171.5 2.2 copy-start.7
  176.3 0.7 copy-start.14
  177.0 4.7 %copy-start.9 = (bf16[320,768]{1,0:T(8,128)(2,1)S(1)}, bf16[320,768]{1,0:T(8,128)(2,1)}, u32[]{:S(2)}) copy-start(bf16[320,768]{1,0:T(8,128)(2,1)} %fusion.49) | copy-start | bytes 1474564
  185.5 4.0 %copy-start = (bf16[1024,1664]{1,0:T(8,128)(2,1)S(1)}, bf16[1024,1664]{1,0:T(8,128)(2,1)}, u32[]{:S(2)}) copy-start(bf16[1024,1664]{1,0:T(8,128)(2,1)} %convolution_convert_fusion) | copy-start | bytes 10223620
  214.2 18.2 %copy-start.3 = (f32[384,1024]{1,0:T(8,128)S(1)}, f32[384,1024]{1,0:T(8,128)}, u32[]{:S(2)}) copy-start(f32[384,1024]{1,0:T(8,128)} %get-tuple-element.35) | copy-start | bytes 4718596

commit v5 on v4

--- a/solution.py
+++ b/solution.py
@@ -106,6 +106,10 @@
 
     half_y = split_y // 2
     half = split_x * half_y
+    over = [(i, (i + half_y) % split_y) for i in range(split_y)]
+    early = max(128, width // 6 // 128 * 128)
+    first = max(2 * early, 2 * width // 3 // 128 * 128)
+    mirror_early = lax.ppermute(features[:, :early], "gy", over)
     at_half = lax.axis_index("gy") // half_y
 
     ids = jnp.concatenate([hop2_ids.reshape(-1), hop1_ids.reshape(-1)])
@@ -131,12 +135,10 @@
     request = jnp.concatenate([request] * 4, axis=1)
     asked = exchange(request, half, (8, lanes), True, half_y, 1, 0)
 
-    first = max(128, 2 * width // 3 // 128 * 128)
-    over = [(i, (i + half_y) % split_y) for i in range(split_y)]
-    asked, sent = lax.optimization_barrier((asked, features[:, :first]))
+    slots = owners * cap + place
+    asked, sent, slots = lax.optimization_barrier((asked, features[:, early:first], slots))
     mirror_first = lax.ppermute(sent, "gy", over)
 
-    slots = owners * cap + place
     far_slots = slots[:far_total].reshape(near_total, fan_two)
     near_slots = slots[far_total:]
 
@@ -154,14 +156,15 @@
         )
         return rows.reshape(half * cap, columns)
 
+    asked, picks = lax.optimization_barrier((asked, (pick(0), pick(1))))
     rows_own = answer(asked, 0, features, 1)
     rows_own, sent = lax.optimization_barrier((rows_own, features[:, first:]))
     mirror_last = lax.ppermute(sent, "gy", over)
-    rows_first = answer(asked, 1, mirror_first, 2)
+    rows_first = answer(asked, 1, jnp.concatenate([mirror_early, mirror_first], axis=1), 2)
     rows_first, asked = lax.optimization_barrier((rows_first, asked))
     rows_last = answer(asked, 1, mirror_last, 6)
-    picked = matmul(pick(0), rows_own) + jnp.concatenate(
-        [matmul(pick(1), rows_first), matmul(pick(1), rows_last)], axis=1
+    picked = matmul(picks[0], rows_own) + jnp.concatenate(
+        [matmul(picks[1], rows_first), matmul(picks[1], rows_last)], axis=1
     )
     near_rows = picked[:near_total].astype(bf16)
     pooled_far = (picked[near_total:] / fan_two).astype(bf16)

time: 236 us -> 208 us (0.88)
  waiting for transfers between devices: 56.7 us -> 0.01 us
  Pallas kernels: 120 us -> 139 us
  starting transfers between devices: 2.45 us -> 8.53 us
  local copies, waits for them, and re-layouts: 9.47 us -> 12.9 us
    ppermute x1, waiting for transfers between devices: 56.7 us -> 0.01 us  [body(): mirror_first = lax.ppermute(sent, 'gy', over)]
    pallas_call x7, Pallas kernels: 120 us -> 139 us  [exchange(): pl.pallas_call(functools.partial(exchange_kernel, wide, count, stride, so...]
    ppermute x1, starting transfers between devices: 2.37 us -> 6.16 us  [body(): mirror_last = lax.ppermute(sent, 'gy', over)]
  transfers between devices with their start and end apart: 2 -> 3, of which waited for: 1 -> 0; matrix products, arithmetic and copies ran while one was open for 6% -> 11% of each run, Pallas kernels for 11% -> 38%
where the time goes in v5:
time: 208 us; the launch traced here: 205 us
  Pallas kernels  139 us (67%)
  matrix products  27.6 us (13%)
  other arithmetic  16.1 us (8%)
  local copies, waits for them, and re-layouts  12.9 us (6%)
  starting transfers between devices  8.53 us (4%)
    pallas_call x7, Pallas kernels, exchange(): pl.pallas_call(functools.partial(exchange_kernel, wide, count, stride, so...  139 us
    dot_general x10, matrix products, matmul(): return jnp.dot(left, right, preferred_element_type=jnp.float32)  23.8 us
    ppermute x1, starting transfers between devices, body(): mirror_last = lax.ppermute(sent, 'gy', over)  6.16 us
  transfers between devices with their start and end apart: 3, of which 0 were waited for; matrix products, arithmetic and copies ran while one was open for 11% of the time, Pallas kernels for 38%

profile of v5, /device:TPU:11, one launch (start us, length us, event | category | flops | bytes accessed | tf_op | source)
XLA Modules:
  0.0 205.3 jit_solution(15125865135834745823)
XLA Ops:
  0.7 0.9 copy.15
  2.8 1.8 fusion.38
  5.8 6.7 %shard_map.111 = s32[16,8,128]{2,1,0:T(8,128)} custom-call(s32[16,8,128]{2,1,0:T(8,128)} %pad_add_fusion.x_ref), custom_call_target="tpu_custom_call" | custom-call | tf_op jit(solution)/shard_map/pallas_call | solution.py:68
  12.5 1.0 slice.84
  13.5 2.3 %collective-permute-start.1 = (bf16[1024,384]{1,0:T(8,128)(2,1)}, bf16[1024,384]{1,0:T(8,128)(2,1)}, u32[]{:S(2)}, u32[]{:S(2)}) collective-permute-start(bf16[1024,384]{1,0:T(8,128)(2,1)} %slice.84), channel_id=1, source_target_pairs={{0,4},{1,5},{2,6},{3,7},{4,0},{5,1},{6,2},{7,3},{8,12},{9,13},{10,... | collective-permute-start | bytes 2359304 | tf_op jit(solution)/shard_map/ppermute | solution.py:140
  16.6 0.8 slice.94
  18.9 2.5 %add_convert_fusion = (bf16[320,1536]{1,0:T(8,128)(2,1)S(1)}, bf16[320,1536]{1,0:T(8,128)(2,1)S(1)}) fusion(s32[1536]{0:T(1024)S(1)} %iota_add_fusion, s32[320]{0:T(512)S(1)} %get-tuple-element.25, s32[320]{0:T(512)S(1)} %get-tuple-element.26, s32[320]{0:T(512)S(1)} %get-tuple-element.27, s32[320]{0:T(512)S(1)} %get-tuple-element.28, ...), kind=kLoop, calls=%fused_computation.28 | loop fusion | flops 14745600 | bytes 1978624 | tf_op jit(solution)/shard_map/convert_element_type | solution.py:149
  21.5 1.4 pad_maximum_fusion
  22.9 1.0 slice_reduce_fusion.7
  24.6 4.8 %fusion.9 = bf16[1536,768]{1,0:T(8,128)(2,1)} fusion(bf16[1024,768]{1,0:T(8,128)(2,1)S(1)} %copy-done.1, s32[1536]{0:T(1024)} %eq.299), kind=kOutput, calls=%fused_computation.14 | convolution fusion | flops 2418671616 | bytes 3938304 | tf_op jit(solution)/shard_map/dot_general | solution.py:87
  29.4 49.7 %shard_map.112 = bf16[16,96,768]{2,1,0:T(8,128)(2,1)} custom-call(bf16[16,96,768]{2,1,0:T(8,128)(2,1)} %bitcast.36), custom_call_target="tpu_custom_call" | custom-call | tf_op jit(solution)/shard_map/pallas_call | solution.py:68
  79.1 6.2 %collective-permute-start.2 = (bf16[1024,256]{1,0:T(8,128)(2,1)}, bf16[1024,256]{1,0:T(8,128)(2,1)}, u32[]{:S(2)}, u32[]{:S(2)}) collective-permute-start(bf16[1024,256]{1,0:T(8,128)(2,1)} %slice.94), channel_id=1, source_target_pairs={{0,4},{1,5},{2,6},{3,7},{4,0},{5,1},{6,2},{7,3},{8,12},{9,13},{10,... | collective-permute-start | bytes 1572872 | tf_op jit(solution)/shard_map/ppermute | solution.py:162
  85.2 1.1 convolution_convert_fusion.1
  86.3 0.9 multiply_convert_fusion
  87.5 1.1 reshape.341
  88.6 4.3 %fusion.17 = bf16[1536,512]{1,0:T(8,128)(2,1)} fusion(s32[1536]{0:T(1024)S(1)} %eq.303, bf16[1024,384]{1,0:T(8,128)(2,1)} %collective-permute-done.1, bf16[1024,128]{1,0:T(8,128)(2,1)} %collective-permute-done), kind=kOutput, calls=%fused_computation.22 | convolution fusion | flops 1615069184 | bytes 2627584 | tf_op jit(solution)/shard_map/dot_general | solution.py:87
  92.9 29.0 %shard_map.113 = bf16[16,96,512]{2,1,0:T(8,128)(2,1)} custom-call(bf16[16,96,512]{2,1,0:T(8,128)(2,1)} %bitcast.38), custom_call_target="tpu_custom_call" | custom-call | tf_op jit(solution)/shard_map/pallas_call | solution.py:68
  122.0 0.9 slice_reduce_fusion.6
  122.9 3.3 %fusion.18 = bf16[1536,256]{1,0:T(8,128)(2,1)} fusion(bf16[1024,256]{1,0:T(8,128)(2,1)} %collective-permute-done.2, s32[1536]{0:T(1024)S(1)} %eq.307), kind=kOutput, calls=%fused_computation.23 | convolution fusion | flops 807272448 | bytes 1316864 | tf_op jit(solution)/shard_map/dot_general | solution.py:87
  126.3 16.7 %shard_map.114 = bf16[16,96,256]{2,1,0:T(8,128)(2,1)} custom-call(bf16[16,96,256]{2,1,0:T(8,128)(2,1)} %bitcast.40), custom_call_target="tpu_custom_call" | custom-call | tf_op jit(solution)/shard_map/pallas_call | solution.py:68
  143.0 1.2 fusion.86
  144.9 1.0 copy-done.2
  146.4 1.7 maximum_add_fusion
  149.2 4.5 %fusion.46 = (f32[384,1024]{1,0:T(8,128)}, f32[384,1024]{1,0:T(8,128)S(1)}) fusion(f32[1024]{0:T(1024)S(1)} %copy-done.12, bf16[768,1024]{1,0:T(8,128)(2,1)} %param.13, bf16[768,1024]{1,0:T(8,128)(2,1)} %param.12, bf16[320,768]{1,0:T(8,128)(2,1)S(1)} %fusion.44, bf16[64,768]{1,0:T(8,128)(2,1)S(1)} %multiply_convert_fusion.1, ...), kind=kOutput, calls=%fused_computation.66 | convolution fusion | flops 1220542464 | bytes 7475200 | tf_op jit(solution)/shard_map/dot_general | solution.py:87
  153.7 3.8 %convolution_convert_fusion = bf16[1024,1664]{1,0:T(8,128)(2,1)} fusion(bf16[320,768]{1,0:T(8,128)(2,1)S(1)} %fusion.44, bf16[64,768]{1,0:T(8,128)(2,1)S(1)} %multiply_convert_fusion.1, bf16[320,768]{1,0:T(8,128)(2,1)S(1)} %slice.145, bf16[64,768]{1,0:T(8,128)(2,1)S(1)} %copy-done.10, f32[384,1024]{1,0:T(8,128)S(1)} %get-tuple-element.45, ...), kind=kOutput, calls=%fused_computation.11 | convolution fusion | flops 1319469056 | bytes 6954240 | tf_op jit(solution)/shard_map/dot_general | solution.py:191
  157.5 4.0 %shard_map.115 = bf16[1,4,4,32,1664]{4,3,2,1,0:T(8,128)(2,1)} custom-call(bf16[4,4,2,32,1664]{4,3,2,1,0:T(8,128)(2,1)} %bitcast.33), custom_call_target="tpu_custom_call" | custom-call | tf_op jit(solution)/shard_map/pallas_call | solution.py:68
  161.5 3.1 %fusion.8.x_ref = bf16[4,4,32,1664]{3,2,1,0:T(8,128)(2,1)} fusion(bf16[1,4,4,32,1664]{4,3,2,1,0:T(8,128)(2,1)} %shard_map.115, bf16[4,4,2,32,1664]{4,3,2,1,0:T(8,128)(2,1)S(1)} %bitcast.34, s32[]{:T(128)S(6)} %select_n.100), kind=kLoop, calls=%fused_computation.13 | loop fusion | flops 3407872 | bytes 5111812 | tf_op jit(solution)/shard_map/convert_element_type | solution.py:214
  164.6 21.7 %shard_map.116 = bf16[4,4,32,1664]{3,2,1,0:T(8,128)(2,1)} custom-call(bf16[4,4,32,1664]{3,2,1,0:T(8,128)(2,1)} %fusion.8.x_ref), custom_call_target="tpu_custom_call" | custom-call | tf_op jit(solution)/shard_map/pallas_call | solution.py:68
  186.3 2.7 %reduce_sum.51.x_ref = bf16[4,32,1664]{2,1,0:T(8,128)(2,1)} reduce(bf16[4,4,32,1664]{3,2,1,0:T(8,128)(2,1)} %shard_map.116, bf16[]{:T(256)} %constant.133.clone.1), dimensions={0}, to_apply=%region_3.4 | reduce | flops 638976 | bytes 2129922 | tf_op jit(solution)/shard_map/reduce_sum | solution.py:216
  189.0 11.3 %shard_map.117 = bf16[4,32,1664]{2,1,0:T(8,128)(2,1)} custom-call(bf16[4,32,1664]{2,1,0:T(8,128)(2,1)} %reduce_sum.51.x_ref), custom_call_target="tpu_custom_call" | custom-call | tf_op jit(solution)/shard_map/pallas_call | solution.py:68
  200.3 1.1 convert_reduce_fusion
  203.7 1.6 fusion.56
  (64 shorter events, 10.4 us)
Async XLA Ops:
  2.8 9.7 %copy-start.1 = (bf16[1024,768]{1,0:T(8,128)(2,1)S(1)}, bf16[1024,768]{1,0:T(8,128)(2,1)}, u32[]{:S(2)}) copy-start(bf16[1024,768]{1,0:T(8,128)(2,1)} %param.8) | copy-start | bytes 4718596
  13.5 75.2 %collective-permute-start.1 = (bf16[1024,384]{1,0:T(8,128)(2,1)}, bf16[1024,384]{1,0:T(8,128)(2,1)}, u32[]{:S(2)}, u32[]{:S(2)}) collective-permute-start(bf16[1024,384]{1,0:T(8,128)(2,1)} %slice.84), channel_id=1, source_target_pairs={{0,4},{1,5},{2,6},{3,7},{4,0},{5,1},{6,2},{7,3},{8,12},{9,13},{10,... | collective-permute-start | bytes 2359304 | tf_op jit(solution)/shard_map/ppermute | solution.py:140
  16.5 72.1 %collective-permute-start = (bf16[1024,128]{1,0:T(8,128)(2,1)}, bf16[1024,128]{1,0:T(8,128)(2,1)}, u32[]{:S(2)}, u32[]{:S(2)}) collective-permute-start(bf16[1024,128]{1,0:T(8,128)(2,1)} %slice.96), channel_id=1, source_target_pairs={{0,4},{1,5},{2,6},{3,7},{4,0},{5,1},{6,2},{7,3},{8,12},{9,13},{10,... | collective-permute-start | bytes 786440 | tf_op jit(solution)/shard_map/ppermute | solution.py:112
  29.4 55.9 %copy-start.11 = (s32[64]{0:T(128)S(1)}, s32[64]{0:T(128)}, u32[]{:S(2)}) copy-start(s32[64]{0:T(128)} %param.9) | copy-start | bytes 772
  79.1 43.8 %collective-permute-start.2 = (bf16[1024,256]{1,0:T(8,128)(2,1)}, bf16[1024,256]{1,0:T(8,128)(2,1)}, u32[]{:S(2)}, u32[]{:S(2)}) collective-permute-start(bf16[1024,256]{1,0:T(8,128)(2,1)} %slice.94), channel_id=1, source_target_pairs={{0,4},{1,5},{2,6},{3,7},{4,0},{5,1},{6,2},{7,3},{8,12},{9,13},{10,... | collective-permute-start | bytes 1572872 | tf_op jit(solution)/shard_map/ppermute | solution.py:162
  87.2 5.7 %copy-start.8 = (bf16[64,1024]{1,0:T(8,128)(2,1)}, bf16[64,1024]{1,0:T(8,128)(2,1)S(1)}, u32[]{:S(2)}) copy-start(bf16[64,1024]{1,0:T(8,128)(2,1)S(1)} %multiply_convert_fusion) | copy-start | bytes 393220
  122.9 20.1 %copy-start.5 = (bf16[16,96,512]{2,1,0:T(8,128)(2,1)S(1)}, bf16[16,96,512]{2,1,0:T(8,128)(2,1)}, u32[]{:S(2)}) copy-start(bf16[16,96,512]{2,1,0:T(8,128)(2,1)} %shard_map.113) | copy-start | bytes 4718596
  143.0 1.2 copy-start.6
  144.2 1.7 copy-start.2
  144.2 2.2 %copy-start.3 = (bf16[640,1536]{1,0:T(8,128)(2,1)S(1)}, bf16[640,1536]{1,0:T(8,128)(2,1)}, u32[]{:S(2)}) copy-start(bf16[640,1536]{1,0:T(8,128)(2,1)} %pad_maximum_fusion) | copy-start | bytes 5898244
  148.3 0.9 copy-start.10
  148.3 0.9 copy-start.12
  149.2 4.5 %copy-start.7 = (bf16[320,1024]{1,0:T(8,128)(2,1)S(1)}, bf16[320,1024]{1,0:T(8,128)(2,1)}, u32[]{:S(2)}) copy-start(bf16[320,1024]{1,0:T(8,128)(2,1)} %reshape.341) | copy-start | bytes 1966084
  149.2 4.5 %copy-start.9 = (bf16[64,1024]{1,0:T(8,128)(2,1)S(1)}, bf16[64,1024]{1,0:T(8,128)(2,1)}, u32[]{:S(2)}) copy-start(bf16[64,1024]{1,0:T(8,128)(2,1)} %copy-done.8) | copy-start | bytes 393220
  157.5 4.0 %copy-start = (bf16[1024,1664]{1,0:T(8,128)(2,1)S(1)}, bf16[1024,1664]{1,0:T(8,128)(2,1)}, u32[]{:S(2)}) copy-start(bf16[1024,1664]{1,0:T(8,128)(2,1)} %convolution_convert_fusion) | copy-start | bytes 10223620
  186.3 16.4 %copy-start.4 = (f32[384,1024]{1,0:T(8,128)S(1)}, f32[384,1024]{1,0:T(8,128)}, u32[]{:S(2)}) copy-start(f32[384,1024]{1,0:T(8,128)} %get-tuple-element.44) | copy-start | bytes 4718596
